TPU v7x, 128 devices: a whole 4x4x4 slice. The times are simulated.
128 devices in a mesh: tbit: 4 (over x), box: 32 (over y, z, core).
Axes of the slice: x: 4, y: 4, z: 4, core: 2. Of those that a mesh axis runs over, the one named last changes fastest.
Arguments:
- coeffs: float32 [64, 64, 4, 64, 256], P(None, 'box', 'tbit'), may hold values from -6 to 6
- skeleton_first: int32 [64, 64, 4, 64], P(None, 'box'), may hold values from 0 to 4095, as said below
- skeleton_second: int32 [64, 64, 4, 64], P(None, 'box'), may hold values from 0 to 8191, as said below
- skeleton_third: int32 [64, 64, 4, 64], P(None, 'box'), may hold values from 0 to 16383, as said below
- checks_first: int32 [128, 64], replicated, may hold values from 0 to 8191, as said below
- checks_second: int32 [256, 64], replicated, may hold values from 0 to 4095, as said below
- checks_third: int32 [512, 64], replicated, may hold values from 0 to 2047, as said below
- ranks_first: int32 [64, 64, 4], P(None, 'box', 'tbit'), may hold values from 32 to 64
- ranks_second: int32 [64, 64, 4], P(None, 'box', 'tbit'), may hold values from 32 to 64
- ranks_third: int32 [64, 4, 2, 32], replicated, may hold values from 32 to 64
- interpolants: float32 [3, 64, 64], replicated, may hold values from -0.09375 to 0.09375
- owners: int32 [4, 64], replicated, may hold values from 0 to 31, as said below
Outputs:
- switched: float32 [4, 32, 2, 4, 32, 64, 256], P('tbit', 'box')
Inputs may be any that keep to these rules, and one draw needn't show every extreme that they name: `skeleton_first`: entry r lies in the r-th of 64 equal parts of its source box of 4096 points. `skeleton_second`: entry r lies in the r-th of 64 equal parts of its source box of 8192 points. `skeleton_third`: entry r lies in the r-th of 64 equal parts of its source box of 16384 points. `checks_first`: entry r lies in the r-th of 64 equal parts of its target box. `checks_second`: entry r lies in the r-th of 64 equal parts of its target box. `checks_third`: entry r lies in the r-th of 64 equal parts of its target box. `owners`: in each row no box index is named more than 4 times, and some index exactly 4 times.
All inputs are finite; a program needn't handle non-finite values.
Results may differ from a plain program's by a relative error of at most 0.0003.
Values sent between devices are 32-bit elements; how exact they have to be, the bound alone decides.
A program may use at most 128 MiB of HBM per device.

v0:
```python
import math

import jax
import jax.numpy as jnp
from jax import lax
from jax.sharding import PartitionSpec as P

NPTS = 1048576


two_pi = 2.0 * math.pi
highest = lax.Precision.HIGHEST


def swapped(value, axis, bit):
    mask = 2**bit
    pairs = [(source, source ^ mask) for source in range(lax.axis_size(axis))]
    return lax.ppermute(value, axis, pairs)


def kernel_block(targets, sources):
    target_rows = targets[..., :, None]
    source_cols = sources[..., None, :]
    upper_part = target_rows // 1024
    lower_part = target_rows % 1024
    phases = (upper_part * source_cols % 1024 * 1024 + lower_part * source_cols) % NPTS
    return jnp.cos(phases.astype(jnp.float32) * (two_pi / NPTS))


def slot_table(owner_row, box_count, capacity):
    parent_count = owner_row.shape[0]
    onehot = (owner_row[:, None] == jnp.arange(box_count, dtype=jnp.int32)[None, :]).astype(
        jnp.int32
    )
    earlier = jnp.cumsum(onehot, axis=0, dtype=jnp.int32) - onehot
    slot_of = jnp.sum(earlier * onehot, axis=1, dtype=jnp.int32)
    matches = (onehot.T[:, None, :] == 1) & (
        slot_of[None, None, :] == jnp.arange(capacity, dtype=jnp.int32)[None, :, None]
    )
    slot_parent = jnp.sum(
        jnp.where(matches, jnp.arange(parent_count, dtype=jnp.int32)[None, None, :], 0), axis=2
    )
    slot_used = jnp.any(matches, axis=2)
    return (slot_parent, slot_used)


def pick_slot(values, position):
    return lax.dynamic_index_in_dim(values, position, 2, keepdims=False)


def partner_level(
    mine_coeffs, mine_points, other_points, targets_both, matrix, rank_rows, swap_bit, mine_child
):
    rank_width = matrix.shape[0]
    parent_count = mine_coeffs.shape[0]
    arrived = swapped(mine_coeffs, "tbit", swap_bit)
    my_targets = lax.dynamic_index_in_dim(
        targets_both.reshape(parent_count, 2, rank_width), mine_child, 1, keepdims=False
    )
    kernels = kernel_block(
        my_targets[:, None, :], jnp.concatenate([mine_points, other_points], axis=2)
    )
    images = jnp.einsum(
        "ahcs,ahsn->ahcn",
        kernels,
        jnp.concatenate([mine_coeffs, arrived], axis=2),
        precision=highest,
    )
    merged = jnp.einsum("ij,ahjn->ahin", matrix, images, precision=highest)
    live_rows = jnp.arange(rank_width, dtype=jnp.int32)[None, None, :] < rank_rows[:, :, None]
    return jnp.where(live_rows[..., None], merged, 0.0)


def per_device(
    coeffs,
    skeleton_first,
    skeleton_second,
    skeleton_third,
    checks_first,
    checks_second,
    checks_third,
    ranks_first,
    ranks_second,
    ranks_third,
    interpolants,
    owners,
):
    tbit_index = lax.axis_index("tbit")
    box_index = lax.axis_index("box")
    box_count = lax.axis_size("box")
    parent_count = coeffs.shape[0]
    rank_width = coeffs.shape[3]
    capacity = 2 * parent_count // box_count
    group_count = 2 * box_count
    local_boxes = 2 * box_index + jnp.arange(2, dtype=jnp.int32)[None, :, None, None]
    four_slots = jnp.arange(4, dtype=jnp.int32)[None, None, :, None]
    points_first = (4 * local_boxes + 2 * (four_slots % 2) + four_slots // 2) * (
        NPTS // (4 * group_count)
    ) + skeleton_first
    points_second = (2 * local_boxes + four_slots % 2) * (
        NPTS // (2 * group_count)
    ) + skeleton_second
    points_third = local_boxes * (NPTS // group_count) + skeleton_third
    targets_first = (
        jnp.arange(2 * parent_count, dtype=jnp.int32)[:, None] * (NPTS // (2 * parent_count))
        + checks_first
    )
    targets_second = (
        jnp.arange(4 * parent_count, dtype=jnp.int32)[:, None] * (NPTS // (4 * parent_count))
        + checks_second
    )
    targets_third = (
        jnp.arange(8 * parent_count, dtype=jnp.int32)[:, None] * (NPTS // (8 * parent_count))
        + checks_third
    )
    partner_high = jnp.bitwise_xor(tbit_index, 2)
    partner_low = jnp.bitwise_xor(tbit_index, 1)
    merged_one = partner_level(
        coeffs[:, :, 0],
        pick_slot(points_first, tbit_index),
        pick_slot(points_first, partner_high),
        targets_first.reshape(parent_count, 2 * rank_width),
        interpolants[0],
        ranks_first[:, :, 0],
        1,
        tbit_index // 2,
    )
    second_targets = lax.dynamic_index_in_dim(
        targets_second.reshape(parent_count, 2, 2 * rank_width), tbit_index // 2, 1, keepdims=False
    )
    merged_two = partner_level(
        merged_one,
        pick_slot(points_second, tbit_index),
        pick_slot(points_second, partner_low),
        second_targets,
        interpolants[1],
        ranks_second[:, :, 0],
        0,
        tbit_index % 2,
    )
    third_points = pick_slot(points_third, tbit_index)
    targets_mine = lax.dynamic_index_in_dim(
        targets_third.reshape(parent_count, 4, 2 * rank_width), tbit_index, 1, keepdims=False
    )
    slot_parent, slot_used = slot_table(
        lax.dynamic_index_in_dim(owners, tbit_index, 0, keepdims=False), box_count, capacity
    )
    rank_mine = lax.dynamic_index_in_dim(ranks_third, tbit_index, 1, keepdims=False)
    parent_rows = slot_parent.T
    used_rows = slot_used.T
    kernels = kernel_block(targets_mine, third_points.reshape(parent_count, 2 * rank_width))
    images = jnp.einsum(
        "acs,asn->acn",
        kernels,
        merged_two.reshape(parent_count, 2 * rank_width, merged_two.shape[-1]),
        precision=highest,
    )
    images = images.reshape(parent_count, 2, rank_width, images.shape[-1])
    merged = jnp.einsum("ij,atjn->tain", interpolants[2], images, precision=highest)
    own_ranks = lax.dynamic_index_in_dim(rank_mine, box_index, 2, keepdims=False)
    live_rows = jnp.arange(rank_width, dtype=jnp.int32)[None, None, :] < own_ranks.T[:, :, None]
    merged = jnp.where(live_rows[..., None], merged, 0.0)
    outgoing = jnp.take(merged, parent_rows, axis=1)
    outgoing = jnp.where(used_rows[None, :, :, None, None], outgoing, 0.0)
    switched = lax.all_to_all(outgoing, "box", split_axis=2, concat_axis=2, tiled=True)
    return switched[None, None]


def solution(mesh):
    return jax.shard_map(
        per_device,
        mesh=mesh,
        in_specs=(
            P(None, "box", "tbit", None, None),
            P(None, "box", None, None),
            P(None, "box", None, None),
            P(None, "box", None, None),
            P(),
            P(),
            P(),
            P(None, "box", "tbit"),
            P(None, "box", "tbit"),
            P(),
            P(),
            P(),
        ),
        out_specs=P("tbit", "box", None, None, None, None, None),
        check_vma=False,
    )
```

profile of v0, /device:TPU:1, one launch (start us, length us, event | category | flops | bytes accessed | tf_op | source)
XLA Modules:
  0.0 710.9 jit_solution(16670101948653421337)
XLA Ops:
  0.0 3.6 collective-permute-start
  3.6 0.8 copy.58
  4.3 0.8 copy.59
  5.5 1.1 broadcast_add_fusion
  6.5 0.1 constant_dynamic-slice_fusion.1
  6.6 0.1 pad_add_fusion.1
  6.8 0.1 iota_compare_fusion
  7.0 176.6 %collective-permute-done = f32[64,2,64,256]{3,2,1,0:T(8,128)} collective-permute-done((f32[64,2,64,256]{3,2,1,0:T(8,128)}, f32[64,2,64,256]{3,2,1,0:T(8,128)}, u32[]{:S(2)}, u32[]{:S(2)}) %collective-permute-start) | collective-permute-done | bytes 8388640 | tf_op jit(solution)/shard_map/ppermute | solution.py:18
  183.6 31.2 %fusion = f32[64,2,64,256]{3,2,1,0:T(8,128)S(1)} fusion(f32[64,2,64,256]{3,2,1,0:T(8,128)} %collective-permute-done, f32[64,2,64,256]{3,2,1,0:T(8,128)} %bitcast.75, s32[64,64]{1,0:T(8,128)S(1)} %get-tuple-element.14, s32[64,2,128]{2,1,0:T(2,128)S(1)} %pad_add_fusion.1, s32[64,64]{1,0:T(8,128)S(1)} %get-tuple-element.13), kind=kOutput, calls=%fused_computation.1 | convolution fusion | flops 3254779904 | bytes 25264128 | tf_op jit(solution)/shard_map/ahcs,ahsn->ahcn/dot_general | solution.py:63
  214.8 9.8 %select_bitcast_fusion = f32[64,2,64,256]{3,2,1,0:T(8,128)} fusion(pred[64,2,64]{2,1,0:T(4,128)(4,1)S(1)} %iota_compare_fusion, f32[64,2,64,256]{3,2,1,0:T(8,128)S(1)} %fusion, f32[3,64,64]{2,1,0:T(8,128)S(1)} %copy-done.4), kind=kOutput, calls=%fused_computation.13 | convolution fusion | flops 1612709888 | bytes 16842752 | tf_op jit(solution)/shard_map/ij,ahjn->ahin/dot_general | solution.py:69
  224.6 1.6 collective-permute-start.1
  226.3 0.7 fusion.98
  227.2 0.2 select_reduce_fusion
  227.4 0.2 fusion.80
  227.8 0.2 and_reduce_fusion
  228.1 1.2 fusion.81
  230.0 0.1 copy.55
  230.1 0.1 reshape.529
  230.4 0.1 broadcast_add_fusion.1
  230.5 0.1 constant_dynamic-slice_fusion.4
  230.7 0.1 pad_add_fusion
  230.8 0.1 iota_compare_fusion.2
  230.9 0.1 iota_compare_fusion.1
  231.2 174.4 %collective-permute-done.1 = f32[64,2,64,256]{3,2,1,0:T(8,128)} collective-permute-done((f32[64,2,64,256]{3,2,1,0:T(8,128)}, f32[64,2,64,256]{3,2,1,0:T(8,128)}, u32[]{:S(2)}, u32[]{:S(2)}) %collective-permute-start.1) | collective-permute-done | bytes 8388640 | tf_op jit(solution)/shard_map/ppermute | solution.py:18
  405.5 31.1 %fusion.4 = f32[64,2,64,256]{3,2,1,0:T(8,128)S(1)} fusion(f32[64,2,64,256]{3,2,1,0:T(8,128)} %collective-permute-done.1, f32[64,2,64,256]{3,2,1,0:T(8,128)} %select_bitcast_fusion, s32[64,64]{1,0:T(8,128)S(1)} %get-tuple-element.12, s32[64,2,128]{2,1,0:T(2,128)S(1)} %pad_add_fusion, s32[64,64]{1,0:T(8,128)S(1)} %get-tuple-element.11), kind=kOutput, calls=%fused_computation.5 | convolution fusion | flops 3254779904 | bytes 25264128 | tf_op jit(solution)/shard_map/ahcs,ahsn->ahcn/dot_general | solution.py:63
  436.6 8.4 %broadcast_select_fusion = f32[64,2,256,64]{2,3,1,0:T(8,128)S(1)} fusion(pred[64,2,64]{2,1,0:T(4,128)(4,1)S(1)} %iota_compare_fusion.1, f32[64,2,64,256]{3,2,1,0:T(8,128)S(1)} %fusion.4, f32[3,64,64]{2,1,0:T(8,128)S(1)} %copy-done.4), kind=kOutput, calls=%fused_computation.60 | convolution fusion | flops 1612709888 | bytes 16842752 | tf_op jit(solution)/shard_map/ij,ahjn->ahin/dot_general | solution.py:69
  445.0 32.3 %fusion.16 = f32[64,128,256]{2,1,0:T(8,128)S(1)} fusion(f32[64,128,256]{2,1,0:T(8,128)S(1)} %bitcast.60, s32[64,128]{1,0:T(8,128)S(1)} %get-tuple-element.10, s32[64,128]{1,0:T(8,128)S(1)} %mul.189, s32[64,128]{1,0:T(8,128)S(1)} %get-tuple-element.9), kind=kOutput, calls=%fused_computation.44 | convolution fusion | flops 3250585600 | bytes 16875520 | tf_op jit(solution)/shard_map/acs,asn->acn/dot_general | solution.py:152
  477.4 10.0 %bitcast_select_fusion = f32[2,64,64,256]{3,2,0,1:T(8,128)} fusion(pred[2,64,64]{2,0,1:T(4,128)(4,1)S(1)} %iota_compare_fusion.2, f32[64,2,64,256]{3,2,1,0:T(8,128)S(1)} %bitcast.61, f32[3,64,64]{2,1,0:T(8,128)S(1)} %copy-done.4), kind=kOutput, calls=%fused_computation.12 | convolution fusion | flops 1612709888 | bytes 16842752 | tf_op jit(solution)/shard_map/ij,atjn->tain/dot_general | solution.py:159
  487.4 13.6 %gather_fusion = f32[128,2,64,256]{3,2,1,0:T(8,128)} fusion(f32[2,64,64,256]{3,2,0,1:T(8,128)} %bitcast_select_fusion, s32[1024]{0:T(1024)S(1)} %pad_clamp_fusion), kind=kCustom, calls=%fused_computation | custom fusion | bytes 33554944 | tf_op jit(solution)/shard_map/jit(_take)/gather | solution.py:163
  501.0 7.7 %fusion.9 = f32[2,4,32,64,256]{4,3,1,0,2:T(8,128)S(1)} fusion(f32[4,32,2,64,256]{4,3,2,1,0:T(8,128)} %bitcast.58, pred[4,32]{0,1:T(8,128)(4,1)S(1)} %copy.52, pred[4,32]{0,1:T(8,128)(4,1)S(1)} %copy.53), kind=kLoop, calls=%fused_computation.11 | loop fusion | flops 8388608 | bytes 33554688 | tf_op jit(solution)/shard_map/jit(_where)/select_n | solution.py:164
  508.7 196.0 %all_to_all.5 = f32[2,4,32,64,256]{4,3,1,0,2:T(8,128)S(1)} all-to-all(f32[2,4,32,64,256]{4,3,1,0,2:T(8,128)S(1)} %fusion.9), channel_id=1, replica_groups=mesh['tbit'=4,'box'=32] {'box'}, dimensions={2} | all-to-all | bytes 33554432 | tf_op jit(solution)/shard_map/all_to_all | solution.py:165
  704.7 6.2 copy.61
  (50 shorter events, 1.7 us)
Async XLA Ops:
  0.0 226.2 %copy-start = (s32[64,4,2,32]{0,3,2,1:T(8,128)S(1)}, s32[64,4,2,32]{0,3,2,1:T(8,128)}, u32[]{:S(2)}) copy-start(s32[64,4,2,32]{0,3,2,1:T(8,128)} %param.21) | copy-start | bytes 196612
  0.0 183.6 %collective-permute-start = (f32[64,2,64,256]{3,2,1,0:T(8,128)}, f32[64,2,64,256]{3,2,1,0:T(8,128)}, u32[]{:S(2)}, u32[]{:S(2)}) collective-permute-start(f32[64,2,64,256]{3,2,1,0:T(8,128)} %bitcast.74), channel_id=1, source_target_pairs={{0,64},{32,96},{64,0},{96,32},{1,65},{33,97},{65,1},{97,33},{2,66}... | collective-permute-start | bytes 25165832 | tf_op jit(solution)/shard_map/ppermute | solution.py:18
  183.6 31.2 %copy-start.4 = (f32[3,64,64]{2,1,0:T(8,128)S(1)}, f32[3,64,64]{2,1,0:T(8,128)}, u32[]{:S(2)}) copy-start(f32[3,64,64]{2,1,0:T(8,128)} %param.22) | copy-start | bytes 147460
  214.8 13.3 %copy-start.6 = (s32[64,2,1]{0,2,1:T(1,128)S(1)}, s32[64,2,1]{0,2,1:T(1,128)}, u32[]{:S(2)}) copy-start(s32[64,2,1]{0,2,1:T(1,128)} %param.20) | copy-start | bytes 1540
  214.8 14.7 %copy-start.5 = (s32[256,64]{0,1:T(8,128)S(1)}, s32[256,64]{0,1:T(8,128)}, u32[]{:S(2)}) copy-start(s32[256,64]{0,1:T(8,128)} %param.17) | copy-start | bytes 196612
  214.8 15.1 %copy-start.3 = (s32[512,64]{0,1:T(8,128)S(1)}, s32[512,64]{0,1:T(8,128)}, u32[]{:S(2)}) copy-start(s32[512,64]{0,1:T(8,128)} %param.18) | copy-start | bytes 393220
  214.8 15.6 %copy-start.2 = (s32[64,2,4,64]{3,2,1,0:T(4,128)S(1)}, s32[64,2,4,64]{3,2,1,0:T(4,128)}, u32[]{:S(2)}) copy-start(s32[64,2,4,64]{3,2,1,0:T(4,128)} %param.14) | copy-start | bytes 393220
  224.6 180.9 %collective-permute-start.1 = (f32[64,2,64,256]{3,2,1,0:T(8,128)}, f32[64,2,64,256]{3,2,1,0:T(8,128)}, u32[]{:S(2)}, u32[]{:S(2)}) collective-permute-start(f32[64,2,64,256]{3,2,1,0:T(8,128)} %select_bitcast_fusion), channel_id=1, source_target_pairs={{0,32},{32,0},{64,96},{96,64},{1,33},{33,1},{65,97},{97,65},{2,34}... | collective-permute-start | bytes 25165832 | tf_op jit(solution)/shard_map/ppermute | solution.py:18
  704.7 6.2 copy-start.1
where the time goes:
time: 711 us
  waiting for transfers between devices  351 us (49%)
  blocking collectives  196 us (28%)
  matrix products  123 us (17%)
  local copies, waits for them, and re-layouts  23.7 us (3%)
  other arithmetic  11.8 us (2%)
    ppermute x2, waiting for transfers between devices, swapped(): return lax.ppermute(value, axis, pairs)  351 us
    all_to_all x1, blocking collectives, per_device(): lax.all_to_all(outgoing, 'box', split_axis=2, concat_axis=2, tiled=True)  196 us
    dot_general x2, matrix products, partner_level(): jnp.einsum('ahcs,ahsn->ahcn', kernels, jnp.concatenate([mine_coeffs, arri...  62.3 us
    dot_general x1, matrix products, per_device(): jnp.einsum('acs,asn->acn', kernels, merged_two.reshape(parent_count, 2 *...  32.3 us
    dot_general x2, matrix products, partner_level(): merged = jnp.einsum('ij,ahjn->ahin', matrix, images, precision=highest)  18.2 us
  transfers between devices with their start and end apart: 2, of which 2 were waited for; matrix products, arithmetic and copies ran while one was open for 1% of the time, Pallas kernels for 0%

commit v1 on v0

v1 whole, which is shorter than its diff:
```python
import functools

import jax
import jax.numpy as jnp
import numpy as np
from jax import lax
from jax.experimental import pallas as pl
from jax.experimental.pallas import tpu as pltpu
from jax.sharding import PartitionSpec as P

NPTS = 1048576
R = 64
A0 = 64
HALF_A = 32
LANES = 128
CAP = 4
MESH = pl.DeviceIdType.MESH
f32 = jnp.float32
bf16 = jnp.bfloat16

SIN_COEFFS = (
    6.2831851600873945,
    -41.34165503088491,
    81.60100403766654,
    -76.54978142785076,
    39.53669915281796,
)

CHIP_STEPS = (
    (1, 0), (0, 1), (3, 0), (0, 3), (1, 1), (3, 3), (1, 3), (3, 1),
    (2, 1), (1, 2), (2, 3), (3, 2), (2, 0), (0, 2), (2, 2),
)


def split(value):
    high = value.astype(bf16)
    low = (value - high.astype(f32)).astype(bf16)
    return high, low


def dot(left, right):
    return jnp.dot(left, right, preferred_element_type=f32)


def dot3(left, right):
    return dot(left[0], right[0]) + dot(left[1], right[0]) + dot(left[0], right[1])


def cosines(scaled_rows, columns):
    phases = (scaled_rows * columns).astype(f32)
    turn = 0.25 - jnp.abs(phases) * (2.0**-32)
    square = turn * turn
    total = SIN_COEFFS[4]
    for coeff in SIN_COEFFS[3::-1]:
        total = total * square + coeff
    return total * turn


def operators_kernel(cols_ref, rows_ref, mats_ref, high_ref, low_ref, q12, q33, mask4, mask2):
    @pl.when(pl.program_id(0) == 0)
    def _():
        zero = jnp.zeros((R, R), f32)

        def pair(first, second):
            return jnp.concatenate(
                [jnp.concatenate([first, zero], axis=1), jnp.concatenate([zero, second], axis=1)],
                axis=0,
            )

        for ref, first, second in ((q12, 0, 1), (q33, 2, 2)):
            high, low = split(pair(mats_ref[first], mats_ref[second]))
            ref[0] = high
            ref[1] = low
        row4 = lax.broadcasted_iota(jnp.int32, (256, 256), 0) // R
        col4 = lax.broadcasted_iota(jnp.int32, (256, 256), 1) // R
        mask4[...] = jnp.where(row4 == col4, 1.0, 0.0).astype(bf16)
        row2 = lax.broadcasted_iota(jnp.int32, (128, 256), 0) // R
        col2 = lax.broadcasted_iota(jnp.int32, (128, 256), 1) // LANES
        mask2[...] = jnp.where(row2 == col2, 1.0, 0.0).astype(bf16)

    rank_row = lax.broadcasted_iota(jnp.int32, (R, 256), 0)
    half_row = lax.broadcasted_iota(jnp.int32, (LANES, LANES), 0)
    for target in range(2):
        x12 = jnp.broadcast_to(rows_ref[0, 2 * target : 2 * target + 1, :], (LANES, LANES)).T
        x3 = jnp.broadcast_to(rows_ref[0, 2 * target + 1 : 2 * target + 2, :], (LANES, LANES)).T
        x12 = jnp.concatenate([x12, x12], axis=1)
        k1 = cosines(x12[:R], cols_ref[0, 0:1, :])
        k2 = cosines(x12[R:], cols_ref[0, 1 + target : 2 + target, :])
        k3 = cosines(x3, cols_ref[0, 3:4, target * LANES : (target + 1) * LANES])
        mixed = dot3((q12[0], q12[1]), split(jnp.concatenate([k1, k2], axis=0)))
        live1 = rank_row < cols_ref[0, 4 + target : 5 + target, :]
        live2 = rank_row < cols_ref[0, 6 + target : 7 + target, :]
        first = split(jnp.where(live1, mixed[:R], 0.0))
        second = split(jnp.where(live2, mixed[R:], 0.0))
        blocks = tuple(jnp.concatenate([part] * 4, axis=0) * mask4[...] for part in first)
        merged = split(dot3(second, blocks))
        stacked = tuple(jnp.concatenate([part] * 2, axis=0) * mask2[...] for part in merged)
        third = dot3((q33[0], q33[1]), split(k3))
        rank3 = jnp.where(
            half_row < R,
            rows_ref[0, 4 + 2 * target : 5 + 2 * target, :],
            rows_ref[0, 5 + 2 * target : 6 + 2 * target, :] + R,
        )
        third = split(jnp.where(half_row < rank3, third, 0.0))
        high, low = split(dot3(third, stacked))
        high_ref[0, target] = high
        low_ref[0, target] = low


def build_operators(cols, rows, mats):
    shape = jax.ShapeDtypeStruct((A0, 2, LANES, 256), bf16)
    block = pl.BlockSpec((1, 2, LANES, 256), lambda a: (a, 0, 0, 0))
    return pl.pallas_call(
        operators_kernel,
        grid=(A0,),
        out_shape=(shape, shape),
        in_specs=[
            pl.BlockSpec((1, 8, 256), lambda a: (a, 0, 0)),
            pl.BlockSpec((1, 8, LANES), lambda a: (a, 0, 0)),
            pl.BlockSpec((3, R, R), lambda a: (0, 0, 0)),
        ],
        out_specs=(block, block),
        scratch_shapes=[
            pltpu.VMEM((2, LANES, LANES), bf16),
            pltpu.VMEM((2, LANES, LANES), bf16),
            pltpu.VMEM((256, 256), bf16),
            pltpu.VMEM((LANES, 256), bf16),
        ],
        cost_estimate=pl.CostEstimate(
            flops=5_000_000_000, bytes_accessed=17_000_000, transcendentals=0
        ),
    )(cols, rows, mats)


def peer_of(box, step):
    row = lax.rem(box // 8 + step // 8, 4)
    col = lax.rem((box // 2) % 4 + (step // 2) % 4, 4)
    core = lax.rem(box % 2 + step % 2, 2)
    return row * 8 + col * 2 + core


def exchange_kernel(
    coeffs, near_even, near_odd, high, low, parents, used, out,
    w_high, w_low, own, near_a, near_b, partial, stage,
    send_a0, send_a1, send_b0, send_b1, recv_a0, recv_a1, recv_b0, recv_b1,
    load_sem, own_sem, near_send, near_recv, part_send, part_recv, msg_send, msg_recv, self_sem,
):
    tbit = lax.axis_index("tbit")
    box = lax.axis_index("box")
    by_low = tbit + 1 - 2 * (tbit % 2)
    by_both = 3 - tbit
    sends = ((send_a0, send_a1), (send_b0, send_b1))
    recvs = ((recv_a0, recv_a1), (recv_b0, recv_b1))

    def eight(group):
        return pl.ds(pl.multiple_of(group * 8, 8), 8)

    def load_operator(group):
        rows = eight(group)
        return (
            pltpu.make_async_copy(high.at[rows], w_high.at[rows], load_sem.at[0, group]),
            pltpu.make_async_copy(low.at[rows], w_low.at[rows], load_sem.at[1, group]),
        )

    def load_own(half, group):
        rows = eight(group)
        lanes = pl.ds(half * LANES, LANES)
        return pltpu.make_async_copy(
            coeffs.at[rows, :, :, lanes], own.at[rows], own_sem.at[half, group]
        )

    def load_near(group):
        side = near_even if group < 4 else near_odd
        return pltpu.make_async_copy(
            side.at[pl.ds((group % 4) * 8, 8)],
            near_a.at[pl.ds(group * 8, 8)],
            load_sem.at[2, group],
        )

    for group in range(8):
        for copy in load_operator(group):
            copy.start()
        load_own(0, group).start()
        load_near(group).start()

    barrier = pltpu.get_barrier_semaphore()

    def greet(step, _):
        pl.semaphore_signal(
            barrier, inc=1, device_id=(tbit, peer_of(box, step)), device_id_type=MESH
        )
        return 0

    lax.fori_loop(1, 32, greet, 0)
    for side in (by_low, by_both):
        pl.semaphore_signal(barrier, inc=1, device_id=(side, box), device_id_type=MESH)
    pl.semaphore_wait(barrier, 33)

    def send_near(group):
        upper = group // 4
        rows = eight(group)
        return pltpu.make_async_remote_copy(
            src_ref=coeffs.at[rows, :, :, pl.ds(LANES, LANES)],
            dst_ref=near_b.at[rows],
            send_sem=near_send.at[group],
            recv_sem=near_recv.at[group],
            device_id=((1 - upper) * by_low + upper * by_both, box),
            device_id_type=MESH,
        )

    def send_partial(half, t, group):
        upper = group // 4
        rows = eight(group)
        return pltpu.make_async_remote_copy(
            src_ref=sends[half][t].at[rows],
            dst_ref=recvs[half][t].at[rows],
            send_sem=part_send.at[half, t, group],
            recv_sem=part_recv.at[half, t, group],
            device_id=((1 - upper) * by_both + upper * by_low, box),
            device_id_type=MESH,
        )

    def multiply(half, near, group):
        def one(member, _):
            a = group * 8 + member
            points = split(
                jnp.concatenate([own[a, 0], near[a, 0], own[a, 1], near[a, 1]], axis=0)
            )
            left = (w_high[a].reshape(256, 256), w_low[a].reshape(256, 256))
            result = dot3(left, points)
            partial[a] = result[:LANES].reshape(2, R, LANES)
            sends[half][0][a] = result[LANES : LANES + R]
            sends[half][1][a] = result[LANES + R :]
            return 0

        lax.fori_loop(0, 8, one, 0)

    def message(half, t, step):
        return pltpu.make_async_remote_copy(
            src_ref=stage.at[t, step],
            dst_ref=out.at[t, :, box, :, pl.ds(half * LANES, LANES)],
            send_sem=msg_send.at[half, t, step],
            recv_sem=msg_recv.at[half, t, step],
            device_id=(tbit, peer_of(box, step)),
            device_id_type=MESH,
        )

    def keep(half, t):
        return pltpu.make_async_copy(
            stage.at[t, 0],
            out.at[t, :, box, :, pl.ds(half * LANES, LANES)],
            self_sem.at[half, t],
        )

    def fill(half, t, step):
        owner = peer_of(box, step)
        for slot in range(CAP):
            parent = parents[owner * CAP + slot]
            live = used[owner * CAP + slot]
            value = partial[parent, t] + recvs[half][t][parent]
            stage[t, step, slot] = jnp.where(jnp.full((R, LANES), live) > 0, value, 0.0)

    def release(half, t):
        for group in range(8):
            send_partial(half, t, group).wait_recv()
        if half == 1:
            keep(0, t).wait()

        def go(step):
            if half == 1:
                message(0, t, step).wait_send()
            fill(half, t, step)
            message(half, t, step).start()

        go(1)
        for core in range(2):
            for row, col in CHIP_STEPS:
                go(row * 8 + col * 2 + core)
        fill(half, t, 0)
        keep(half, t).start()

    for group in range(8):
        for copy in load_operator(group):
            copy.wait()
        load_own(0, group).wait()
        load_near(group).wait()
        multiply(0, near_a, group)
        load_own(1, group).start()
        send_partial(0, 0, group).start()
    for group in range(8):
        send_partial(0, 1, group).start()
    for group in range(8):
        send_near(group).start()
    release(0, 0)
    release(0, 1)

    for group in range(8):
        load_own(1, group).wait()
        send_near(group).wait_recv()
        multiply(1, near_b, group)
        send_partial(1, 0, group).start()
    for group in range(8):
        send_partial(1, 1, group).start()
    release(1, 0)
    release(1, 1)

    for t in range(2):
        keep(1, t).wait()

        def finish(step, _):
            message(1, t, step).wait_send()
            message(0, t, step).wait_recv()
            message(1, t, step).wait_recv()
            return 0

        lax.fori_loop(1, 32, finish, 0)
    for group in range(8):
        send_near(group).wait_send()
        for half in range(2):
            for t in range(2):
                send_partial(half, t, group).wait_send()


def exchange(coeffs, near_even, near_odd, high, low, parents, used):
    hbm = pl.BlockSpec(memory_space=pl.ANY)
    smem = pl.BlockSpec(memory_space=pltpu.SMEM)
    part = pltpu.VMEM((A0, R, LANES), f32)
    halves = pltpu.VMEM((A0, 2, R, LANES), f32)
    dma = pltpu.SemaphoreType.DMA
    return pl.pallas_call(
        exchange_kernel,
        out_shape=jax.ShapeDtypeStruct((2, CAP, 32, R, 256), f32),
        in_specs=[hbm] * 5 + [smem] * 2,
        out_specs=hbm,
        scratch_shapes=[
            pltpu.VMEM((A0, 2, LANES, 256), bf16),
            pltpu.VMEM((A0, 2, LANES, 256), bf16),
            halves, halves, halves, halves,
            pltpu.VMEM((2, 32, CAP, R, LANES), f32),
        ]
        + [part] * 8
        + [
            dma((3, 8)), dma((2, 8)), dma((8,)), dma((8,)),
            dma((2, 2, 8)), dma((2, 2, 8)), dma((2, 2, 32)), dma((2, 2, 32)), dma((2, 2)),
        ],
        compiler_params=pltpu.CompilerParams(
            collective_id=0, has_side_effects=True, vmem_limit_bytes=62 << 20
        ),
    )(coeffs, near_even, near_odd, high, low, parents, used)


def slot_table(owner_row, box_count, capacity):
    parent_count = owner_row.shape[0]
    onehot = (owner_row[:, None] == jnp.arange(box_count, dtype=jnp.int32)[None, :]).astype(
        jnp.int32
    )
    earlier = jnp.cumsum(onehot, axis=0, dtype=jnp.int32) - onehot
    slot_of = jnp.sum(earlier * onehot, axis=1, dtype=jnp.int32)
    matches = (onehot.T[:, None, :] == 1) & (
        slot_of[None, None, :] == jnp.arange(capacity, dtype=jnp.int32)[None, :, None]
    )
    slot_parent = jnp.sum(
        jnp.where(matches, jnp.arange(parent_count, dtype=jnp.int32)[None, None, :], 0), axis=2
    )
    slot_used = jnp.any(matches, axis=2)
    return (slot_parent, slot_used)


def by_parent(values, axis, even, odd):
    return jnp.concatenate(
        [
            lax.dynamic_index_in_dim(values[:HALF_A], even, axis, keepdims=False),
            lax.dynamic_index_in_dim(values[HALF_A:], odd, axis, keepdims=False),
        ],
        axis=0,
    )


def tables(
    tbit, box, skeleton_first, skeleton_second, skeleton_third,
    checks_first, checks_second, checks_third, ranks_first, ranks_second, ranks_third,
):
    local_boxes = 2 * box + jnp.arange(2, dtype=jnp.int32)[None, :, None, None]
    four = jnp.arange(4, dtype=jnp.int32)[None, None, :, None]
    points_first = (4 * local_boxes + 2 * (four % 2) + four // 2) * (NPTS // 256) + skeleton_first
    points_second = (2 * local_boxes + four % 2) * (NPTS // 128) + skeleton_second
    points_third = local_boxes * (NPTS // 64) + skeleton_third
    parent = jnp.arange(A0, dtype=jnp.int32)
    low, high, both = tbit ^ 1, tbit ^ 2, tbit ^ 3
    group = tbit // 2
    ranks = jnp.moveaxis(
        lax.all_gather(jnp.stack([ranks_first[:, :, 0], ranks_second[:, :, 0]]), "tbit"), 0, -1
    )

    def wide(values):
        return jnp.broadcast_to(values, (A0, 2, 2, R)).reshape(A0, 256)

    def both_sources(values, axis, first, second):
        return jnp.stack(
            [by_parent(values, axis, *first), by_parent(values, axis, *second)], axis=2
        )

    own, other = (tbit, tbit), (both, low)
    first_slots = ((tbit, tbit), (low, low))
    other_slots = ((high, tbit), (both, low))
    row0 = both_sources(points_first, 2, (tbit, tbit), (low, both)).reshape(A0, 256)
    row1 = both_sources(points_second, 2, *first_slots).reshape(A0, 256)
    row2 = both_sources(points_second, 2, *other_slots).reshape(A0, 256)
    row3 = jnp.concatenate(
        [by_parent(points_third, 2, *side).reshape(A0, 128) for side in (own, other)], axis=1
    )
    row4 = wide(both_sources(ranks[0], 2, *first_slots)[..., None])
    row5 = wide(both_sources(ranks[0], 2, *other_slots)[..., None])
    row6 = wide(by_parent(ranks[1], 2, *own)[:, :, None, None])
    row7 = wide(by_parent(ranks[1], 2, *other)[:, :, None, None])
    columns = jnp.stack([row0, row1, row2, row3, row4, row5, row6, row7], axis=1)

    targets_first = (
        jnp.arange(2 * A0, dtype=jnp.int32)[:, None] * (NPTS // (2 * A0)) + checks_first
    ).reshape(A0, 2, R)
    targets_second = (
        jnp.arange(4 * A0, dtype=jnp.int32)[:, None] * (NPTS // (4 * A0)) + checks_second
    ).reshape(A0, 4, R)
    targets_third = (
        jnp.arange(8 * A0, dtype=jnp.int32)[:, None] * (NPTS // (8 * A0)) + checks_third
    ).reshape(A0, 4, 2 * R)
    ranks_mine = lax.dynamic_index_in_dim(ranks_third, box, 3, keepdims=False)
    rows, limits = [], []
    for side, groups in ((own, (group, group)), (other, (1 - group, group))):
        rows.append(
            jnp.concatenate(
                [by_parent(targets_first, 1, *groups), by_parent(targets_second, 1, *side)],
                axis=1,
            )
            * 4096
        )
        rows.append(by_parent(targets_third, 1, *side) * 4096)
        limit = by_parent(ranks_mine, 1, *side)
        limits += [jnp.broadcast_to(limit[:, t : t + 1], (A0, LANES)) for t in range(2)]
    return columns, jnp.stack(rows + limits, axis=1)


def per_device(
    coeffs,
    skeleton_first,
    skeleton_second,
    skeleton_third,
    checks_first,
    checks_second,
    checks_third,
    ranks_first,
    ranks_second,
    ranks_third,
    interpolants,
    owners,
):
    tbit = lax.axis_index("tbit")
    box = lax.axis_index("box")
    coeffs = coeffs[:, :, 0]
    near_even = lax.ppermute(
        coeffs[:HALF_A, :, :, :LANES], "tbit", [(k, k ^ 1) for k in range(4)]
    )
    near_odd = lax.ppermute(
        coeffs[HALF_A:, :, :, :LANES], "tbit", [(k, k ^ 3) for k in range(4)]
    )
    columns, rows = tables(
        tbit, box, skeleton_first, skeleton_second, skeleton_third,
        checks_first, checks_second, checks_third, ranks_first, ranks_second, ranks_third,
    )
    high, low = build_operators(columns, rows, interpolants)
    slot_parent, slot_used = slot_table(
        lax.dynamic_index_in_dim(owners, tbit, 0, keepdims=False), 32, CAP
    )
    switched = exchange(
        coeffs, near_even, near_odd, high, low,
        slot_parent.reshape(-1), slot_used.reshape(-1).astype(jnp.int32),
    )
    return switched[None, None]


def solution(mesh):
    return jax.shard_map(
        per_device,
        mesh=mesh,
        in_specs=(
            P(None, "box", "tbit", None, None),
            P(None, "box", None, None),
            P(None, "box", None, None),
            P(None, "box", None, None),
            P(),
            P(),
            P(),
            P(None, "box", "tbit"),
            P(None, "box", "tbit"),
            P(),
            P(),
            P(),
        ),
        out_specs=P("tbit", "box", None, None, None, None, None),
        check_vma=False,
    )
```

time: 711 us -> 418 us (0.59)
  waiting for transfers between devices: 351 us -> 0.01 us
  Pallas kernels: 0 us -> 330 us
  blocking collectives: 196 us -> 49.4 us
  matrix products: 123 us -> 0 us
  other arithmetic: 11.8 us -> 2.49 us
    ppermute x2, waiting for transfers between devices: 351 us -> 0.01 us  [the longest x1 0.01 us: per_device(): lax.ppermute(coeffs[HALF_A:, :, :, :LANES], 'tbit', [(k, k ^ 3) for k in...]
    pallas_call x0 -> x2, Pallas kernels: none -> 330 us  [the longest x1 245 us: exchange(): pl.pallas_call(exchange_kernel, out_shape=jax.ShapeDtypeStruct((2, CAP, 3...]
    all_to_all x1 -> x0, blocking collectives: 196 us -> none  [per_device(): lax.all_to_all(outgoing, 'box', split_axis=2, concat_axis=2, tiled=True)]
    dot_general x6 -> x0, matrix products: 123 us -> none  [the longest x2 62.3 us: partner_level(): jnp.einsum('ahcs,ahsn->ahcn', kernels, jnp.concatenate([mine_coeffs, arri...]
    all_gather x0 -> x1, blocking collectives: none -> 49.4 us  [tables(): lax.all_gather(jnp.stack([ranks_first[:, :, 0], ranks_second[:, :, 0]]),...]
    gather x1 -> x0, local copies, waits for them, and re-layouts: 13.6 us -> none  [per_device(): outgoing = jnp.take(merged, parent_rows, axis=1)]
    unnamed x15 -> x23, local copies, waits for them, and re-layouts: 0.88 us -> 12 us
    select_n x6 -> x1, other arithmetic: 7.8 us -> 0.01 us  [tables(): four // 2]
  transfers between devices with their start and end apart: 2 -> 2, of which waited for: 2 -> 0; matrix products, arithmetic and copies ran while one was open for 1% -> 3% of each run, Pallas kernels for 0% -> 21%
where the time goes in v1:
time: 418 us; the launch traced here: 412 us
  Pallas kernels  330 us (79%)
  blocking collectives  49.4 us (12%)
  local copies, waits for them, and re-layouts  26.6 us (6%)
    pallas_call x1, Pallas kernels, exchange(): pl.pallas_call(exchange_kernel, out_shape=jax.ShapeDtypeStruct((2, CAP, 3...  245 us
    pallas_call x1, Pallas kernels, build_operators(): pl.pallas_call(operators_kernel, grid=(A0,), out_shape=(shape, shape), in...  84.8 us
    all_gather x1, blocking collectives, tables(): lax.all_gather(jnp.stack([ranks_first[:, :, 0], ranks_second[:, :, 0]]),...  49.4 us
    unnamed x23, local copies, waits for them, and re-layouts  12 us
  transfers between devices with their start and end apart: 2, of which 0 were waited for; matrix products, arithmetic and copies ran while one was open for 3% of the time, Pallas kernels for 21%

profile of v1, /device:TPU:1, one launch (start us, length us, event | category | flops | bytes accessed | tf_op | source)
XLA Modules:
  0.0 412.1 jit_solution(17060360969559244031)
XLA Ops:
  0.1 4.9 %fusion.19 = (f32[32,2,64,128]{3,2,1,0:T(8,128)}, f32[32,2,64,128]{3,2,1,0:T(8,128)}) fusion(f32[64,2,64,256]{3,2,1,0:T(8,128)} %bitcast.90), kind=kLoop, calls=%fused_computation.118 | loop fusion | bytes 8388608 | tf_op jit(solution)/shard_map/slice | solution.py:464
  4.9 3.3 collective-permute-start.1
  8.5 0.2 select_reduce_fusion
  8.7 0.2 and_reduce_fusion
  8.9 0.2 fusion.2
  9.0 49.4 %all-gather = s32[8,64,2]{1,2,0:T(2,128)S(1)} all-gather(s32[2,64,2]{1,2,0:T(2,128)S(1)} %pad_add_fusion.12), channel_id=2, replica_groups=mesh['tbit'=4,'box'=32] {'tbit'}, dimensions={0}, use_global_device_ids=true | all-gather | bytes 5120 | tf_op jit(solution)/shard_map/all_gather | solution.py:392
  60.2 0.4 dynamic-slice_reduce_fusion.2
  61.4 0.1 pad_add_fusion.2
  61.7 0.1 pad_add_fusion
  61.8 0.9 constant_dynamic-slice_fusion.2
  63.3 0.7 reshape.410.used
  64.0 0.6 reshape.409.parents
  64.8 0.2 broadcast_in_dim.18
  65.0 0.1 stack_reshape.24
  65.3 0.2 broadcast_in_dim.19
  65.5 0.1 stack_reshape.25
  65.7 0.2 broadcast_in_dim.21
  65.9 0.1 stack_reshape.27
  66.1 0.2 broadcast_in_dim.20
  66.3 0.1 stack_reshape.26
  66.4 0.1 stack_reshape.23
  66.7 0.1 stack_reshape.22
  66.9 0.1 stack_reshape.21
  67.3 0.1 add_multiply_fusion.2
  67.7 0.1 stack_broadcast_in_dim.9
  67.8 0.1 stack_broadcast_in_dim.10
  67.9 0.1 stack_broadcast_in_dim.8
  68.1 1.1 stack.79.rows_ref
  69.2 1.5 stack.78.cols_ref
  70.7 84.8 %shard_map.118 = (bf16[64,2,128,256]{3,2,1,0:T(8,128)(2,1)}, bf16[64,2,128,256]{3,2,1,0:T(8,128)(2,1)}) custom-call(s32[64,8,256]{2,1,0:T(8,128)} %stack.78.cols_ref, s32[64,8,128]{2,1,0:T(8,128)} %stack.79.rows_ref, f32[3,64,64]{2,1,0:T(8,128)} %mats_ref.1), custom_call_target="tpu_custom_call" | custom-call | flops 5000000000 | bytes 17000000 | tf_op jit(solution)/shard_map/pallas_call | solution.py:113
  155.5 244.7 %shard_map.119 = f32[2,4,32,64,256]{4,3,2,1,0:T(8,128)} custom-call(f32[64,2,64,256]{3,2,1,0:T(8,128)} %bitcast.91, f32[32,2,64,128]{3,2,1,0:T(8,128)} %collective-permute-done.near_even, f32[32,2,64,128]{3,2,1,0:T(8,128)} %collective-permute-done.1.near_odd, bf16[64,2,128,256]{3,2,1,0:T(8,128)(2,1)} %get-tuple-element.7.high, ...), custom_call_target="tpu_custom_call" | custom-call | tf_op jit(solution)/shard_map/pallas_call | solution.py:330
  400.2 11.8 %copy.75 = f32[1,1,2,4,32,64,256]{6,5,4,3,2,1,0:T(8,128)} copy(f32[1,1,2,4,32,64,256]{6,5,4,3,2,1,0:T(8,128)} %bitcast.89) | data formatting | bytes 33554432
  (103 shorter events, 4.2 us)
Async XLA Ops:
  0.0 8.3 %copy-start = (s32[4,64]{1,0:T(4,128)S(1)}, s32[4,64]{1,0:T(4,128)}, u32[]{:S(2)}) copy-start(s32[4,64]{1,0:T(4,128)} %param.23) | copy-start | bytes 3076
  0.0 9.0 %copy-start.8 = (s32[64,2,1]{0,2,1:T(1,128)S(1)}, s32[64,2,1]{0,2,1:T(1,128)}, u32[]{:S(2)}) copy-start(s32[64,2,1]{0,2,1:T(1,128)} %param.20) | copy-start | bytes 1540
  0.0 9.0 %copy-start.9 = (s32[64,2,1]{0,2,1:T(1,128)S(1)}, s32[64,2,1]{0,2,1:T(1,128)}, u32[]{:S(2)}) copy-start(s32[64,2,1]{0,2,1:T(1,128)} %param.19) | copy-start | bytes 1540
  0.0 58.6 %copy-start.5 = (s32[512,64]{0,1:T(8,128)S(1)}, s32[512,64]{0,1:T(8,128)}, u32[]{:S(2)}) copy-start(s32[512,64]{0,1:T(8,128)} %param.18) | copy-start | bytes 393220
  0.0 59.0 %copy-start.6 = (s32[256,64]{0,1:T(8,128)S(1)}, s32[256,64]{0,1:T(8,128)}, u32[]{:S(2)}) copy-start(s32[256,64]{0,1:T(8,128)} %param.17) | copy-start | bytes 196612
  0.0 59.3 %copy-start.3 = (s32[64,2,4,64]{3,2,1,0:T(4,128)S(1)}, s32[64,2,4,64]{3,2,1,0:T(4,128)}, u32[]{:S(2)}) copy-start(s32[64,2,4,64]{3,2,1,0:T(4,128)} %param.14) | copy-start | bytes 393220
  0.0 59.8 %copy-start.4 = (s32[64,2,4,64]{3,2,1,0:T(4,128)S(1)}, s32[64,2,4,64]{3,2,1,0:T(4,128)}, u32[]{:S(2)}) copy-start(s32[64,2,4,64]{3,2,1,0:T(4,128)} %param.13) | copy-start | bytes 393220
  0.1 60.0 %copy-start.2 = (s32[64,2,4,64]{3,2,1,0:T(4,128)S(1)}, s32[64,2,4,64]{3,2,1,0:T(4,128)}, u32[]{:S(2)}) copy-start(s32[64,2,4,64]{3,2,1,0:T(4,128)} %param.15) | copy-start | bytes 393220
  0.1 65.6 %copy-start.7 = (s32[128,64]{0,1:T(8,128)S(1)}, s32[128,64]{0,1:T(8,128)}, u32[]{:S(2)}) copy-start(s32[128,64]{0,1:T(8,128)} %param.16) | copy-start | bytes 98308
  4.9 150.5 %collective-permute-start.1 = (f32[32,2,64,128]{3,2,1,0:T(8,128)}, f32[32,2,64,128]{3,2,1,0:T(8,128)}, u32[]{:S(2)}, u32[]{:S(2)}) collective-permute-start(f32[32,2,64,128]{3,2,1,0:T(8,128)} %get-tuple-element.13), channel_id=1, source_target_pairs={{0,96},{32,64},{64,32},{96,0},{1,97},{33,65},{65,33},{97,1},{2,98}... | collective-permute-start | bytes 6291464 | tf_op jit(solution)/shard_map/ppermute | solution.py:463
  8.2 147.2 %collective-permute-start = (f32[32,2,64,128]{3,2,1,0:T(8,128)}, f32[32,2,64,128]{3,2,1,0:T(8,128)}, u32[]{:S(2)}, u32[]{:S(2)}) collective-permute-start(f32[32,2,64,128]{3,2,1,0:T(8,128)} %get-tuple-element.14), channel_id=1, source_target_pairs={{0,32},{32,0},{64,96},{96,64},{1,33},{33,1},{65,97},{97,65},{2,34}... | collective-permute-start | bytes 6291464 | tf_op jit(solution)/shard_map/ppermute | solution.py:460
  400.2 11.8 %copy-start.1 = (s32[4,64]{1,0:T(4,128)S(1)}, s32[4,64]{1,0:T(4,128)}, u32[]{:S(2)}) copy-start(s32[4,64]{1,0:T(4,128)} %param.23) | copy-start | bytes 3076

commit v2 on v1

v2 whole, which is shorter than its diff:
```python
import functools

import jax
import jax.numpy as jnp
import numpy as np
from jax import lax
from jax.experimental import pallas as pl
from jax.experimental.pallas import tpu as pltpu
from jax.sharding import PartitionSpec as P

NPTS = 1048576
R = 64
A0 = 64
HALF_A = 32
LANES = 128
GROUP = 8
BATCH = 8
UNROLL = 4
CAP = 4
MESH = pl.DeviceIdType.MESH
f32 = jnp.float32
bf16 = jnp.bfloat16

SIN_COEFFS = (
    6.2831851600873945,
    -41.34165503088491,
    81.60100403766654,
    -76.54978142785076,
    39.53669915281796,
)

CHIP_STEPS = (
    (1, 0), (0, 1), (3, 0), (0, 3), (1, 1), (3, 3), (1, 3), (3, 1),
    (2, 1), (1, 2), (2, 3), (3, 2), (2, 0), (0, 2), (2, 2),
)

PIECES = ((0, 0, 32), (0, 32, 32), (1, 0, 64))


def split(value):
    high = value.astype(bf16)
    low = (value - high.astype(f32)).astype(bf16)
    return high, low


def dot(left, right):
    return jnp.dot(left, right, preferred_element_type=f32)


def dot3(left, right):
    return dot(left[0], right[0]) + dot(left[1], right[0]) + dot(left[0], right[1])


def cosines(scaled_rows, columns):
    phases = (scaled_rows * columns).astype(f32)
    turn = 0.25 - jnp.abs(phases) * (2.0**-32)
    square = turn * turn
    total = SIN_COEFFS[4]
    for coeff in SIN_COEFFS[3::-1]:
        total = total * square + coeff
    return total * turn


def operators_kernel(cols_ref, rows_ref, mats_ref, high_ref, low_ref, mats, mask4, mask2):
    @pl.when(pl.program_id(0) == 0)
    def _():
        for level in range(3):
            high, low = split(mats_ref[level])
            mats[level] = jnp.concatenate([high, low, high, low], axis=1)
        row4 = lax.broadcasted_iota(jnp.int32, (256, 256), 0) // R
        col4 = lax.broadcasted_iota(jnp.int32, (256, 256), 1) // R
        mask4[...] = jnp.where(row4 == col4, 1.0, 0.0).astype(bf16)
        row2 = lax.broadcasted_iota(jnp.int32, (128, 256), 0) // R
        col2 = lax.broadcasted_iota(jnp.int32, (128, 256), 1) // LANES
        mask2[...] = jnp.where(row2 == col2, 1.0, 0.0).astype(bf16)

    rank_row = lax.broadcasted_iota(jnp.int32, (R, 256), 0)
    rank_half = lax.broadcasted_iota(jnp.int32, (R, LANES), 0)

    def doubled(kernel):
        high, low = split(kernel)
        return jnp.concatenate([high, high, low, low], axis=0)

    def masked(value, member, row):
        return split(jnp.where(rank_row < cols_ref[member, row : row + 1, :], value, 0.0))

    def cut(value, member, row):
        halves = [
            jnp.where(
                rank_half < rows_ref[member, row + t : row + t + 1, :],
                value[:, t * LANES : (t + 1) * LANES],
                0.0,
            )
            for t in range(2)
        ]
        return split(jnp.concatenate(halves, axis=0))

    def batch(units):
        points = []
        for member, target in units:
            x12 = rows_ref[member, 2 * target : 2 * target + 1, :]
            x12 = jnp.broadcast_to(x12, (LANES, LANES)).T
            x3 = rows_ref[member, 2 * target + 1 : 2 * target + 2, :]
            points.append(
                (jnp.concatenate([x12, x12], axis=1), jnp.broadcast_to(x3, (LANES, LANES)).T)
            )
        k1 = [
            doubled(cosines(p[0][:R], cols_ref[m, 0:1, :])) for p, (m, t) in zip(points, units)
        ]
        first = [dot(mats[0], k) for k in k1]
        k2 = [
            doubled(cosines(p[0][R:], cols_ref[m, 1 + t : 2 + t, :]))
            for p, (m, t) in zip(points, units)
        ]
        second = [dot(mats[1], k) for k in k2]
        k3 = [
            cosines(p[1], cols_ref[m, 3:4, t * LANES : (t + 1) * LANES])
            for p, (m, t) in zip(points, units)
        ]
        k3 = [doubled(jnp.concatenate([k[:R], k[R:]], axis=1)) for k in k3]
        third = [dot(mats[2], k) for k in k3]
        first = [masked(v, m, 4 + t) for v, (m, t) in zip(first, units)]
        blocks = [
            tuple(jnp.concatenate([part] * 4, axis=0) * mask4[...] for part in v) for v in first
        ]
        second = [masked(v, m, 6 + t) for v, (m, t) in zip(second, units)]
        merged = [dot(jnp.concatenate(v, axis=0), b[0]) for v, b in zip(second, blocks)]
        extra = [dot(v[0], b[1]) for v, b in zip(second, blocks)]
        third = [cut(v, m, 4 + 2 * t) for v, (m, t) in zip(third, units)]
        merged = [split(v[:R] + v[R:] + e) for v, e in zip(merged, extra)]
        stacked = [
            tuple(jnp.concatenate([part] * 2, axis=0) * mask2[...] for part in v) for v in merged
        ]
        main = [
            dot(jnp.concatenate(v, axis=1), jnp.concatenate([b[0]] * 2, axis=0))
            for v, b in zip(third, stacked)
        ]
        rest = [dot(v[0], b[1]) for v, b in zip(third, stacked)]
        for v, e, (member, target) in zip(main, rest, units):
            high, low = split(v + e)
            high_ref[member, target] = high
            low_ref[member, target] = low

    units = [(m, t) for m in range(GROUP) for t in range(2)]
    for begin in range(0, len(units), BATCH):
        batch(units[begin : begin + BATCH])


def build_operators(cols, rows, mats):
    shape = jax.ShapeDtypeStruct((A0, 2, LANES, 256), bf16)
    block = pl.BlockSpec((GROUP, 2, LANES, 256), lambda a: (a, 0, 0, 0))
    return pl.pallas_call(
        operators_kernel,
        grid=(A0 // GROUP,),
        out_shape=(shape, shape),
        in_specs=[
            pl.BlockSpec((GROUP, 8, 256), lambda a: (a, 0, 0)),
            pl.BlockSpec((GROUP, 8, LANES), lambda a: (a, 0, 0)),
            pl.BlockSpec((3, R, R), lambda a: (0, 0, 0)),
        ],
        out_specs=(block, block),
        scratch_shapes=[
            pltpu.VMEM((3, R, 256), bf16),
            pltpu.VMEM((256, 256), bf16),
            pltpu.VMEM((LANES, 256), bf16),
        ],
        cost_estimate=pl.CostEstimate(
            flops=20_000_000_000, bytes_accessed=17_000_000, transcendentals=0
        ),
    )(cols, rows, mats)


def peer_of(box, step):
    row = lax.rem(box // 8 + step // 8, 4)
    col = lax.rem((box // 2) % 4 + (step // 2) % 4, 4)
    core = lax.rem(box % 2 + step % 2, 2)
    return row * 8 + col * 2 + core


def exchange_kernel(
    coeffs, near_even, near_odd, high, low, parents, used, out,
    w_high, w_low, own, near_a, near_b, partial, *rest,
):
    count = len(PIECES)
    stages, sends, recvs = rest[:count], rest[count : 3 * count], rest[3 * count : 5 * count]
    (
        load_sem, own_sem, near_send, near_recv, part_send, part_recv,
        msg_send, msg_recv, self_sem,
    ) = rest[5 * count :]
    tbit = lax.axis_index("tbit")
    box = lax.axis_index("box")
    by_low = tbit + 1 - 2 * (tbit % 2)
    by_both = 3 - tbit

    def eight(group):
        return pl.ds(group * 8, 8)

    def load_operator(group):
        rows = eight(group)
        return (
            pltpu.make_async_copy(high.at[rows], w_high.at[rows], load_sem.at[0, group]),
            pltpu.make_async_copy(low.at[rows], w_low.at[rows], load_sem.at[1, group]),
        )

    def load_own(half, group):
        rows = eight(group)
        lanes = pl.ds(half * LANES, LANES)
        return pltpu.make_async_copy(
            coeffs.at[rows, :, :, lanes], own.at[rows], own_sem.at[half, group]
        )

    def load_near(group):
        side = near_even if group < 4 else near_odd
        return pltpu.make_async_copy(
            side.at[eight(group % 4)], near_a.at[eight(group)], load_sem.at[2, group]
        )

    for group in range(8):
        for copy in load_operator(group):
            copy.start()
        load_own(0, group).start()
        load_near(group).start()

    barrier = pltpu.get_barrier_semaphore()

    def greet(step, _):
        pl.semaphore_signal(
            barrier, inc=1, device_id=(tbit, peer_of(box, step)), device_id_type=MESH
        )
        return 0

    lax.fori_loop(1, 32, greet, 0)
    for side in (by_low, by_both):
        pl.semaphore_signal(barrier, inc=1, device_id=(side, box), device_id_type=MESH)
    pl.semaphore_wait(barrier, 33)

    def send_near(group):
        rows = eight(group)
        return pltpu.make_async_remote_copy(
            src_ref=coeffs.at[rows, :, :, pl.ds(LANES, LANES)],
            dst_ref=near_b.at[rows],
            send_sem=near_send.at[group],
            recv_sem=near_recv.at[group],
            device_id=(by_low if group < 4 else by_both, box),
            device_id_type=MESH,
        )

    def send_partial(half, piece, group):
        rows = eight(group)
        index = half * count + piece
        return pltpu.make_async_remote_copy(
            src_ref=sends[index].at[rows],
            dst_ref=recvs[index].at[rows],
            send_sem=part_send.at[index, group],
            recv_sem=part_recv.at[index, group],
            device_id=(by_both if group < 4 else by_low, box),
            device_id_type=MESH,
        )

    def multiply(half, near, group):
        def some(batch, _):
            members = [group * 8 + batch * UNROLL + k for k in range(UNROLL)]
            points = [
                split(jnp.concatenate([own[a, 0], near[a, 0], own[a, 1], near[a, 1]], axis=0))
                for a in members
            ]
            highs = [w_high[a].reshape(256, 256) for a in members]
            main = [
                dot(jnp.concatenate([h, w_low[a].reshape(256, 256)], axis=0), p[0])
                for h, a, p in zip(highs, members, points)
            ]
            extra = [dot(h, p[1]) for h, p in zip(highs, points)]
            for a, m, e in zip(members, main, extra):
                result = m[:256] + m[256:] + e
                partial[a] = result[:LANES].reshape(2, R, LANES)
                for piece, (t, begin, size) in enumerate(PIECES):
                    first = LANES + t * R + begin
                    sends[half * count + piece][a] = result[first : first + size]
            return 0

        lax.fori_loop(0, 8 // UNROLL, some, 0)

    def target(half, piece):
        t, begin, size = PIECES[piece]
        return out.at[t, :, box, pl.ds(begin, size), pl.ds(half * LANES, LANES)]

    def message(half, piece, step):
        index = half * count + piece
        return pltpu.make_async_remote_copy(
            src_ref=stages[piece].at[step],
            dst_ref=target(half, piece),
            send_sem=msg_send.at[index, step],
            recv_sem=msg_recv.at[index, step],
            device_id=(tbit, peer_of(box, step)),
            device_id_type=MESH,
        )

    def keep(half, piece):
        return pltpu.make_async_copy(
            stages[piece].at[0], target(half, piece), self_sem.at[half, piece]
        )

    def fill(half, piece, step):
        t, begin, size = PIECES[piece]
        owner = peer_of(box, step)
        for slot in range(CAP):
            parent = parents[owner * CAP + slot]
            live = used[owner * CAP + slot]
            value = partial[parent, t, begin : begin + size]
            value = value + recvs[half * count + piece][parent]
            stages[piece][step, slot] = jnp.where(jnp.full((size, LANES), live) > 0, value, 0.0)

    def release(half, piece):
        for group in range(8):
            send_partial(half, piece, group).wait_recv()
        if half == 1:
            keep(0, piece).wait()

        def go(step):
            if half == 1:
                message(0, piece, step).wait_send()
            fill(half, piece, step)
            message(half, piece, step).start()

        go(1)
        for core in range(2):
            for row, col in CHIP_STEPS:
                go(row * 8 + col * 2 + core)
        fill(half, piece, 0)
        keep(half, piece).start()

    for group in range(8):
        for copy in load_operator(group):
            copy.wait()
        load_own(0, group).wait()
        load_near(group).wait()
        multiply(0, near_a, group)
        load_own(1, group).start()
        send_partial(0, 0, group).start()
    for piece in range(1, count):
        for group in range(8):
            send_partial(0, piece, group).start()
    for group in range(8):
        send_near(group).start()
    for piece in range(count):
        release(0, piece)

    for group in range(8):
        load_own(1, group).wait()
        send_near(group).wait_recv()
        multiply(1, near_b, group)
        send_partial(1, 0, group).start()
    for piece in range(1, count):
        for group in range(8):
            send_partial(1, piece, group).start()
    for piece in range(count):
        release(1, piece)

    for piece in range(count):
        keep(1, piece).wait()

        def finish(step, _):
            message(1, piece, step).wait_send()
            message(0, piece, step).wait_recv()
            message(1, piece, step).wait_recv()
            return 0

        lax.fori_loop(1, 32, finish, 0)
    for group in range(8):
        send_near(group).wait_send()
        for half in range(2):
            for piece in range(count):
                send_partial(half, piece, group).wait_send()


def exchange(coeffs, near_even, near_odd, high, low, parents, used):
    hbm = pl.BlockSpec(memory_space=pl.ANY)
    smem = pl.BlockSpec(memory_space=pltpu.SMEM)
    count = len(PIECES)
    parts = [pltpu.VMEM((A0, size, LANES), f32) for _, _, size in PIECES]
    halves = pltpu.VMEM((A0, 2, R, LANES), f32)
    dma = pltpu.SemaphoreType.DMA
    return pl.pallas_call(
        exchange_kernel,
        out_shape=jax.ShapeDtypeStruct((2, CAP, 32, R, 256), f32),
        in_specs=[hbm] * 5 + [smem] * 2,
        out_specs=hbm,
        scratch_shapes=[
            pltpu.VMEM((A0, 2, LANES, 256), bf16),
            pltpu.VMEM((A0, 2, LANES, 256), bf16),
            halves, halves, halves, halves,
        ]
        + [pltpu.VMEM((32, CAP, size, LANES), f32) for _, _, size in PIECES]
        + parts * 4
        + [
            dma((3, 8)), dma((2, 8)), dma((8,)), dma((8,)),
            dma((2 * count, 8)), dma((2 * count, 8)),
            dma((2 * count, 32)), dma((2 * count, 32)), dma((2, count)),
        ],
        compiler_params=pltpu.CompilerParams(
            collective_id=0, has_side_effects=True, vmem_limit_bytes=62 << 20
        ),
    )(coeffs, near_even, near_odd, high, low, parents, used)


def slot_table(owner_row, box_count, capacity):
    parent_count = owner_row.shape[0]
    onehot = (owner_row[:, None] == jnp.arange(box_count, dtype=jnp.int32)[None, :]).astype(
        jnp.int32
    )
    earlier = jnp.cumsum(onehot, axis=0, dtype=jnp.int32) - onehot
    slot_of = jnp.sum(earlier * onehot, axis=1, dtype=jnp.int32)
    matches = (onehot.T[:, None, :] == 1) & (
        slot_of[None, None, :] == jnp.arange(capacity, dtype=jnp.int32)[None, :, None]
    )
    slot_parent = jnp.sum(
        jnp.where(matches, jnp.arange(parent_count, dtype=jnp.int32)[None, None, :], 0), axis=2
    )
    slot_used = jnp.any(matches, axis=2)
    return (slot_parent, slot_used)


def by_parent(values, axis, even, odd):
    return jnp.concatenate(
        [
            lax.dynamic_index_in_dim(values[:HALF_A], even, axis, keepdims=False),
            lax.dynamic_index_in_dim(values[HALF_A:], odd, axis, keepdims=False),
        ],
        axis=0,
    )


def tables(
    tbit, box, skeleton_first, skeleton_second, skeleton_third,
    checks_first, checks_second, checks_third, ranks, ranks_third,
):
    local_boxes = 2 * box + jnp.arange(2, dtype=jnp.int32)[None, :, None, None]
    four = jnp.arange(4, dtype=jnp.int32)[None, None, :, None]
    points_first = (4 * local_boxes + 2 * (four % 2) + four // 2) * (NPTS // 256) + skeleton_first
    points_second = (2 * local_boxes + four % 2) * (NPTS // 128) + skeleton_second
    points_third = local_boxes * (NPTS // 64) + skeleton_third
    parent = jnp.arange(A0, dtype=jnp.int32)
    low, high, both = tbit ^ 1, tbit ^ 2, tbit ^ 3
    group = tbit // 2

    def wide(values):
        return jnp.broadcast_to(values, (A0, 2, 2, R)).reshape(A0, 256)

    def both_sources(values, axis, first, second):
        return jnp.stack(
            [by_parent(values, axis, *first), by_parent(values, axis, *second)], axis=2
        )

    own, other = (tbit, tbit), (both, low)
    first_slots = ((tbit, tbit), (low, low))
    other_slots = ((high, tbit), (both, low))
    row0 = both_sources(points_first, 2, (tbit, tbit), (low, both)).reshape(A0, 256)
    row1 = both_sources(points_second, 2, *first_slots).reshape(A0, 256)
    row2 = both_sources(points_second, 2, *other_slots).reshape(A0, 256)
    row3 = jnp.concatenate(
        [by_parent(points_third, 2, *side).reshape(A0, 128) for side in (own, other)], axis=1
    )
    mine, by_low, by_high, by_both = ranks

    def halves(even, odd):
        return jnp.concatenate([even[:HALF_A], odd[HALF_A:]], axis=0)

    row4 = wide(jnp.stack([mine[0], by_low[0]], axis=2)[..., None])
    row5 = wide(
        jnp.stack([halves(by_high[0], mine[0]), halves(by_both[0], by_low[0])], axis=2)[..., None]
    )
    row6 = wide(mine[1][:, :, None, None])
    row7 = wide(halves(by_both[1], by_low[1])[:, :, None, None])
    columns = jnp.stack([row0, row1, row2, row3, row4, row5, row6, row7], axis=1)

    targets_first = (
        jnp.arange(2 * A0, dtype=jnp.int32)[:, None] * (NPTS // (2 * A0)) + checks_first
    ).reshape(A0, 2, R)
    targets_second = (
        jnp.arange(4 * A0, dtype=jnp.int32)[:, None] * (NPTS // (4 * A0)) + checks_second
    ).reshape(A0, 4, R)
    targets_third = (
        jnp.arange(8 * A0, dtype=jnp.int32)[:, None] * (NPTS // (8 * A0)) + checks_third
    ).reshape(A0, 4, 2 * R)
    ranks_mine = lax.dynamic_index_in_dim(ranks_third, box, 3, keepdims=False)
    rows, limits = [], []
    for side, groups in ((own, (group, group)), (other, (1 - group, group))):
        rows.append(
            jnp.concatenate(
                [by_parent(targets_first, 1, *groups), by_parent(targets_second, 1, *side)],
                axis=1,
            )
            * 4096
        )
        rows.append(by_parent(targets_third, 1, *side) * 4096)
        limit = by_parent(ranks_mine, 1, *side)
        limits += [jnp.broadcast_to(limit[:, t : t + 1], (A0, LANES)) for t in range(2)]
    return columns, jnp.stack(rows + limits, axis=1)


def per_device(
    coeffs,
    skeleton_first,
    skeleton_second,
    skeleton_third,
    checks_first,
    checks_second,
    checks_third,
    ranks_first,
    ranks_second,
    ranks_third,
    interpolants,
    owners,
):
    tbit = lax.axis_index("tbit")
    box = lax.axis_index("box")
    coeffs = coeffs[:, :, 0]

    def crossed(value, mask):
        return lax.ppermute(value, "tbit", [(k, k ^ mask) for k in range(4)])

    ranks = jnp.stack([ranks_first[:, :, 0], ranks_second[:, :, 0]])
    ranks = (ranks,) + tuple(crossed(ranks, mask) for mask in (1, 2, 3))
    even, odd = coeffs[:HALF_A, :, :, :LANES], coeffs[HALF_A:, :, :, :LANES]
    even, odd, ranks = lax.optimization_barrier((even, odd, ranks))
    near_even = crossed(even, 1)
    near_odd = crossed(odd, 3)
    columns, rows = tables(
        tbit, box, skeleton_first, skeleton_second, skeleton_third,
        checks_first, checks_second, checks_third, ranks, ranks_third,
    )
    high, low = build_operators(columns, rows, interpolants)
    slot_parent, slot_used = slot_table(
        lax.dynamic_index_in_dim(owners, tbit, 0, keepdims=False), 32, CAP
    )
    switched = exchange(
        coeffs, near_even, near_odd, high, low,
        slot_parent.reshape(-1), slot_used.reshape(-1).astype(jnp.int32),
    )
    return switched[None, None]


def solution(mesh):
    return jax.shard_map(
        per_device,
        mesh=mesh,
        in_specs=(
            P(None, "box", "tbit", None, None),
            P(None, "box", None, None),
            P(None, "box", None, None),
            P(None, "box", None, None),
            P(),
            P(),
            P(),
            P(None, "box", "tbit"),
            P(None, "box", "tbit"),
            P(),
            P(),
            P(),
        ),
        out_specs=P("tbit", "box", None, None, None, None, None),
        check_vma=False,
    )
```

time: 418 us -> 306 us (0.73)
  Pallas kernels: 330 us -> 255 us
  blocking collectives: 49.4 us -> 0 us
  waiting for transfers between devices: 0.01 us -> 5.55 us
  other arithmetic: 2.49 us -> 6.96 us
    all_gather x1 -> x0, blocking collectives: 49.4 us -> none  [tables(): lax.all_gather(jnp.stack([ranks_first[:, :, 0], ranks_second[:, :, 0]]),...]
    pallas_call x1, Pallas kernels: 84.8 us -> 36.2 us  [build_operators(): pl.pallas_call(operators_kernel, grid=(A0 // GROUP,), out_shape=(shape, s...]
    pallas_call x1, Pallas kernels: 245 us -> 219 us  [exchange(): pl.pallas_call(exchange_kernel, out_shape=jax.ShapeDtypeStruct((2, CAP, 3...]
    ppermute x2 -> x5, waiting for transfers between devices: 0.01 us -> 5.55 us  [crossed(): return lax.ppermute(value, 'tbit', [(k, k ^ mask) for k in range(4)])]
    unnamed x23 -> x7, local copies, waits for them, and re-layouts: 12 us -> 13.6 us
  transfers between devices with their start and end apart: 2 -> 5, of which waited for: 0 -> 2; matrix products, arithmetic and copies ran while one was open for 3% -> 6% of each run, Pallas kernels for 21% -> 12%
where the time goes in v2:
time: 306 us; the launch traced here: 303 us
  Pallas kernels  255 us (83%)
  local copies, waits for them, and re-layouts  27.4 us (9%)
  starting transfers between devices  7.19 us (2%)
  other arithmetic  6.96 us (2%)
  waiting for transfers between devices  5.55 us (2%)
    pallas_call x1, Pallas kernels, exchange(): pl.pallas_call(exchange_kernel, out_shape=jax.ShapeDtypeStruct((2, CAP, 3...  219 us
    pallas_call x1, Pallas kernels, build_operators(): pl.pallas_call(operators_kernel, grid=(A0 // GROUP,), out_shape=(shape, s...  36.2 us
    unnamed x7, local copies, waits for them, and re-layouts  13.6 us
    ppermute x5, starting transfers between devices, crossed(): return lax.ppermute(value, 'tbit', [(k, k ^ mask) for k in range(4)])  7.19 us
  transfers between devices with their start and end apart: 5, of which 2 were waited for; matrix products, arithmetic and copies ran while one was open for 6% of the time, Pallas kernels for 12%

profile of v2, /device:TPU:1, one launch (start us, length us, event | category | flops | bytes accessed | tf_op | source)
XLA Modules:
  0.0 302.8 jit_solution(4493142505104872561)
XLA Ops:
  0.0 0.7 pad_add_fusion.12
  0.7 3.3 %collective-permute-start.2 = (s32[2,64,2]{1,2,0:T(2,128)S(1)}, s32[2,64,2]{1,2,0:T(2,128)S(1)}, u32[]{:S(2)}, u32[]{:S(2)}) collective-permute-start(s32[2,64,2]{1,2,0:T(2,128)S(1)} %pad_add_fusion.12), channel_id=1, source_target_pairs={{0,96},{32,64},{64,32},{96,0},{1,97},{33,65},{65,33},{97,1},{2,98}... | collective-permute-start | bytes 3080 | tf_op jit(solution)/shard_map/ppermute | solution.py:520
  4.0 0.5 collective-permute-start.1
  4.9 0.2 select_reduce_fusion
  5.1 0.2 and_reduce_fusion
  5.2 0.2 fusion.2
  5.4 0.9 constant_dynamic-slice_fusion.2
  6.3 0.8 copy.48
  7.3 0.9 broadcast_add_fusion.3
  8.6 0.9 copy.49
  9.8 1.1 broadcast_add_fusion.1
  11.0 1.1 broadcast_add_fusion.2
  12.2 1.1 broadcast_add_fusion
  13.3 0.4 dynamic-slice_reduce_fusion.2
  14.1 4.0 %fusion.9 = (f32[32,2,64,128]{3,2,1,0:T(8,128)S(1)}, f32[32,2,64,128]{3,2,1,0:T(8,128)}) fusion(f32[64,2,64,256]{3,2,1,0:T(8,128)} %bitcast.80), kind=kLoop, calls=%fused_computation.103 | loop fusion | bytes 8388608 | tf_op jit(solution)/shard_map/slice | solution.py:524
  19.5 0.7 reshape.392.used
  20.2 0.7 reshape.391.parents
  22.3 0.2 broadcast_in_dim.20
  22.5 0.1 stack_reshape.24
  22.8 0.2 broadcast_in_dim.21
  23.1 0.2 broadcast_in_dim.23
  23.5 0.2 broadcast_in_dim.24
  23.7 0.1 stack_reshape.27
  23.8 1.5 collective-permute-start.3
  25.3 1.8 collective-permute-start.4
  27.7 1.1 stack.71.rows_ref
  28.8 1.5 stack.70.cols_ref
  30.2 36.2 %shard_map.118 = (bf16[64,2,128,256]{3,2,1,0:T(8,128)(2,1)}, bf16[64,2,128,256]{3,2,1,0:T(8,128)(2,1)}) custom-call(s32[64,8,256]{2,1,0:T(8,128)} %stack.70.cols_ref, s32[64,8,128]{2,1,0:T(8,128)} %stack.71.rows_ref, f32[3,64,64]{2,1,0:T(8,128)} %mats_ref.1), custom_call_target="tpu_custom_call" | custom-call | flops 20000000000 | bytes 17000000 | tf_op jit(solution)/shard_map/pallas_call | solution.py:152
  66.4 3.3 %collective-permute-done.3.near_even = f32[32,2,64,128]{3,2,1,0:T(8,128)} collective-permute-done((f32[32,2,64,128]{3,2,1,0:T(8,128)}, f32[32,2,64,128]{3,2,1,0:T(8,128)}, u32[]{:S(2)}, u32[]{:S(2)}) %collective-permute-start.3) | collective-permute-done | bytes 2097184 | tf_op jit(solution)/shard_map/ppermute | solution.py:520
  69.7 2.2 collective-permute-done.4.near_odd
  72.0 219.0 %shard_map.119 = f32[2,4,32,64,256]{4,3,2,1,0:T(8,128)} custom-call(f32[64,2,64,256]{3,2,1,0:T(8,128)} %bitcast.81, f32[32,2,64,128]{3,2,1,0:T(8,128)} %collective-permute-done.3.near_even, f32[32,2,64,128]{3,2,1,0:T(8,128)} %collective-permute-done.4.near_odd, bf16[64,2,128,256]{3,2,1,0:T(8,128)(2,1)} %get-tuple-element.19.high, ...), custom_call_target="tpu_custom_call" | custom-call | tf_op jit(solution)/shard_map/pallas_call | solution.py:383
  291.0 11.8 %copy.57 = f32[1,1,2,4,32,64,256]{6,5,4,3,2,1,0:T(8,128)} copy(f32[1,1,2,4,32,64,256]{6,5,4,3,2,1,0:T(8,128)} %bitcast.79) | data formatting | bytes 33554432
  (92 shorter events, 5.2 us)
Async XLA Ops:
  0.0 4.7 %copy-start = (s32[4,64]{1,0:T(4,128)S(1)}, s32[4,64]{1,0:T(4,128)}, u32[]{:S(2)}) copy-start(s32[4,64]{1,0:T(4,128)} %param.23) | copy-start | bytes 3076
  0.7 20.8 %collective-permute-start.2 = (s32[2,64,2]{1,2,0:T(2,128)S(1)}, s32[2,64,2]{1,2,0:T(2,128)S(1)}, u32[]{:S(2)}, u32[]{:S(2)}) collective-permute-start(s32[2,64,2]{1,2,0:T(2,128)S(1)} %pad_add_fusion.12), channel_id=1, source_target_pairs={{0,96},{32,64},{64,32},{96,0},{1,97},{33,65},{65,33},{97,1},{2,98}... | collective-permute-start | bytes 3080 | tf_op jit(solution)/shard_map/ppermute | solution.py:520
  4.0 17.5 %collective-permute-start.1 = (s32[2,64,2]{1,2,0:T(2,128)S(1)}, s32[2,64,2]{1,2,0:T(2,128)S(1)}, u32[]{:S(2)}, u32[]{:S(2)}) collective-permute-start(s32[2,64,2]{1,2,0:T(2,128)S(1)} %pad_add_fusion.12), channel_id=1, source_target_pairs={{0,64},{32,96},{64,0},{96,32},{1,65},{33,97},{65,1},{97,33},{2,66}... | collective-permute-start | bytes 3080 | tf_op jit(solution)/shard_map/ppermute | solution.py:520
  4.5 17.0 %collective-permute-start = (s32[2,64,2]{1,2,0:T(2,128)S(1)}, s32[2,64,2]{1,2,0:T(2,128)S(1)}, u32[]{:S(2)}, u32[]{:S(2)}) collective-permute-start(s32[2,64,2]{1,2,0:T(2,128)S(1)} %pad_add_fusion.12), channel_id=1, source_target_pairs={{0,32},{32,0},{64,96},{96,64},{1,33},{33,1},{65,97},{97,65},{2,34}... | collective-permute-start | bytes 3080 | tf_op jit(solution)/shard_map/ppermute | solution.py:520
  23.8 45.9 %collective-permute-start.3 = (f32[32,2,64,128]{3,2,1,0:T(8,128)}, f32[32,2,64,128]{3,2,1,0:T(8,128)}, u32[]{:S(2)}, u32[]{:S(2)}) collective-permute-start(f32[32,2,64,128]{3,2,1,0:T(8,128)} %get-tuple-element.13), channel_id=1, source_target_pairs={{0,32},{32,0},{64,96},{96,64},{1,33},{33,1},{65,97},{97,65},{2,34}... | collective-permute-start | bytes 6291464 | tf_op jit(solution)/shard_map/ppermute | solution.py:520
  25.3 46.6 %collective-permute-start.4 = (f32[32,2,64,128]{3,2,1,0:T(8,128)S(1)}, f32[32,2,64,128]{3,2,1,0:T(8,128)}, u32[]{:S(2)}, u32[]{:S(2)}) collective-permute-start(f32[32,2,64,128]{3,2,1,0:T(8,128)S(1)} %get-tuple-element.14), channel_id=1, source_target_pairs={{0,96},{32,64},{64,32},{96,0},{1,97},{33,65},{65,33},{97,1},{2,98}... | collective-permute-start | bytes 6291464 | tf_op jit(solution)/shard_map/ppermute | solution.py:520
  291.0 11.8 %copy-start.1 = (s32[4,64]{1,0:T(4,128)S(1)}, s32[4,64]{1,0:T(4,128)}, u32[]{:S(2)}) copy-start(s32[4,64]{1,0:T(4,128)} %param.23) | copy-start | bytes 3076

commit v3 on v2

--- a/solution.py
+++ b/solution.py
@@ -61,8 +61,84 @@
     return total * turn
 
 
-def operators_kernel(cols_ref, rows_ref, mats_ref, high_ref, low_ref, mats, mask4, mask2):
-    @pl.when(pl.program_id(0) == 0)
+def operators_kernel(
+    ranks, limits, first_ref, second_ref, third_ref, checks1, checks2, checks3, mats_ref,
+    high_ref, low_ref, mats, mask4, mask2,
+):
+    step = pl.program_id(0)
+    tbit = lax.axis_index("tbit")
+    box = lax.axis_index("box")
+    upper = step >= HALF_A // GROUP
+    near = jnp.where(upper, tbit ^ 3, tbit ^ 1)
+    other = jnp.where(upper, tbit ^ 1, tbit ^ 3)
+    targets = (tbit, other)
+    apart = ((0, 1), (jnp.where(upper, 0, 2), jnp.where(upper, 1, 3)))
+    lane_block = lax.broadcasted_iota(jnp.int32, (1, 256), 1) // R
+
+    def first_row(member):
+        return jnp.concatenate(
+            [
+                first_ref[member, h, pl.ds(slot, 1), :]
+                + (4 * (2 * box + h) + 2 * (slot % 2) + slot // 2) * (NPTS // 256)
+                for h in range(2)
+                for slot in (tbit, near)
+            ],
+            axis=1,
+        )
+
+    def second_row(member, target):
+        slots = [tbit ^ distance for distance in apart[target]]
+        return jnp.concatenate(
+            [
+                second_ref[member, h, pl.ds(slot, 1), :]
+                + (2 * (2 * box + h) + slot % 2) * (NPTS // 128)
+                for h in range(2)
+                for slot in slots
+            ],
+            axis=1,
+        )
+
+    def third_row(member, target):
+        return jnp.concatenate(
+            [
+                third_ref[member, h, pl.ds(targets[target], 1), :]
+                + (2 * box + h) * (NPTS // 64)
+                for h in range(2)
+            ],
+            axis=1,
+        )
+
+    def check_rows(member, target):
+        a = step * GROUP + member
+        i = targets[target]
+
+        def points(ref, index, size):
+            return (ref[pl.ds(index, 1), :] + index * size) * 4096
+
+        x12 = [
+            points(checks1, 2 * a + i // 2, NPTS // (2 * A0)),
+            points(checks2, 4 * a + i, NPTS // (4 * A0)),
+        ]
+        x3 = [points(checks3, 8 * a + 2 * i + t, NPTS // (8 * A0)) for t in range(2)]
+        return jnp.concatenate(x12, axis=1), jnp.concatenate(x3, axis=1)
+
+    def rank_of(distance, level, member, h):
+        return ranks[((distance * 2 + level) * A0 + step * GROUP + member) * 2 + h]
+
+    def first_ranks(member, target):
+        near0, near1 = apart[target]
+        row = rank_of(near0, 0, member, 0)
+        for block, (h, distance) in ((1, (0, near1)), (2, (1, near0)), (3, (1, near1))):
+            row = jnp.where(lane_block == block, rank_of(distance, 0, member, h), row)
+        return row
+
+    def second_ranks(member, target):
+        distance = (0, jnp.where(upper, 1, 3))[target]
+        return jnp.where(
+            lane_block < 2, rank_of(distance, 1, member, 0), rank_of(distance, 1, member, 1)
+        )
+
+    @pl.when(step == 0)
     def _():
         for level in range(3):
             high, low = split(mats_ref[level])
@@ -81,13 +157,14 @@
         high, low = split(kernel)
         return jnp.concatenate([high, high, low, low], axis=0)
 
-    def masked(value, member, row):
-        return split(jnp.where(rank_row < cols_ref[member, row : row + 1, :], value, 0.0))
-
-    def cut(value, member, row):
+    def masked(value, row):
+        return split(jnp.where(rank_row < row, value, 0.0))
+
+    def cut(value, member, target):
+        first = ((step * GROUP + member) * 4 + targets[target]) * 2
         halves = [
             jnp.where(
-                rank_half < rows_ref[member, row + t : row + t + 1, :],
+                rank_half < limits[first + t],
                 value[:, t * LANES : (t + 1) * LANES],
                 0.0,
             )
@@ -98,35 +175,34 @@
     def batch(units):
         points = []
         for member, target in units:
-            x12 = rows_ref[member, 2 * target : 2 * target + 1, :]
+            x12, x3 = check_rows(member, target)
             x12 = jnp.broadcast_to(x12, (LANES, LANES)).T
-            x3 = rows_ref[member, 2 * target + 1 : 2 * target + 2, :]
             points.append(
                 (jnp.concatenate([x12, x12], axis=1), jnp.broadcast_to(x3, (LANES, LANES)).T)
             )
         k1 = [
-            doubled(cosines(p[0][:R], cols_ref[m, 0:1, :])) for p, (m, t) in zip(points, units)
+            doubled(cosines(p[0][:R], first_row(m))) for p, (m, t) in zip(points, units)
         ]
         first = [dot(mats[0], k) for k in k1]
         k2 = [
-            doubled(cosines(p[0][R:], cols_ref[m, 1 + t : 2 + t, :]))
+            doubled(cosines(p[0][R:], second_row(m, t)))
             for p, (m, t) in zip(points, units)
         ]
         second = [dot(mats[1], k) for k in k2]
         k3 = [
-            cosines(p[1], cols_ref[m, 3:4, t * LANES : (t + 1) * LANES])
+            cosines(p[1], third_row(m, t))
             for p, (m, t) in zip(points, units)
         ]
         k3 = [doubled(jnp.concatenate([k[:R], k[R:]], axis=1)) for k in k3]
         third = [dot(mats[2], k) for k in k3]
-        first = [masked(v, m, 4 + t) for v, (m, t) in zip(first, units)]
+        first = [masked(v, first_ranks(m, t)) for v, (m, t) in zip(first, units)]
         blocks = [
             tuple(jnp.concatenate([part] * 4, axis=0) * mask4[...] for part in v) for v in first
         ]
-        second = [masked(v, m, 6 + t) for v, (m, t) in zip(second, units)]
+        second = [masked(v, second_ranks(m, t)) for v, (m, t) in zip(second, units)]
         merged = [dot(jnp.concatenate(v, axis=0), b[0]) for v, b in zip(second, blocks)]
         extra = [dot(v[0], b[1]) for v, b in zip(second, blocks)]
-        third = [cut(v, m, 4 + 2 * t) for v, (m, t) in zip(third, units)]
+        third = [cut(v, m, t) for v, (m, t) in zip(third, units)]
         merged = [split(v[:R] + v[R:] + e) for v, e in zip(merged, extra)]
         stacked = [
             tuple(jnp.concatenate([part] * 2, axis=0) * mask2[...] for part in v) for v in merged
@@ -146,18 +222,21 @@
         batch(units[begin : begin + BATCH])
 
 
-def build_operators(cols, rows, mats):
+def build_operators(ranks, limits, first, second, third, checks1, checks2, checks3, mats):
     shape = jax.ShapeDtypeStruct((A0, 2, LANES, 256), bf16)
     block = pl.BlockSpec((GROUP, 2, LANES, 256), lambda a: (a, 0, 0, 0))
+    smem = pl.BlockSpec(memory_space=pltpu.SMEM)
+    points = pl.BlockSpec((GROUP, 2, 4, R), lambda a: (a, 0, 0, 0))
+
+    def whole(array):
+        return pl.BlockSpec(array.shape, lambda a: (0,) * array.ndim)
+
     return pl.pallas_call(
         operators_kernel,
         grid=(A0 // GROUP,),
         out_shape=(shape, shape),
-        in_specs=[
-            pl.BlockSpec((GROUP, 8, 256), lambda a: (a, 0, 0)),
-            pl.BlockSpec((GROUP, 8, LANES), lambda a: (a, 0, 0)),
-            pl.BlockSpec((3, R, R), lambda a: (0, 0, 0)),
-        ],
+        in_specs=[smem, smem, points, points, points]
+        + [whole(array) for array in (checks1, checks2, checks3, mats)],
         out_specs=(block, block),
         scratch_shapes=[
             pltpu.VMEM((3, R, 256), bf16),
@@ -167,7 +246,7 @@
         cost_estimate=pl.CostEstimate(
             flops=20_000_000_000, bytes_accessed=17_000_000, transcendentals=0
         ),
-    )(cols, rows, mats)
+    )(ranks, limits, first, second, third, checks1, checks2, checks3, mats)
 
 
 def peer_of(box, step):
@@ -420,84 +499,6 @@
     return (slot_parent, slot_used)
 
 
-def by_parent(values, axis, even, odd):
-    return jnp.concatenate(
-        [
-            lax.dynamic_index_in_dim(values[:HALF_A], even, axis, keepdims=False),
-            lax.dynamic_index_in_dim(values[HALF_A:], odd, axis, keepdims=False),
-        ],
-        axis=0,
-    )
-
-
-def tables(
-    tbit, box, skeleton_first, skeleton_second, skeleton_third,
-    checks_first, checks_second, checks_third, ranks, ranks_third,
-):
-    local_boxes = 2 * box + jnp.arange(2, dtype=jnp.int32)[None, :, None, None]
-    four = jnp.arange(4, dtype=jnp.int32)[None, None, :, None]
-    points_first = (4 * local_boxes + 2 * (four % 2) + four // 2) * (NPTS // 256) + skeleton_first
-    points_second = (2 * local_boxes + four % 2) * (NPTS // 128) + skeleton_second
-    points_third = local_boxes * (NPTS // 64) + skeleton_third
-    parent = jnp.arange(A0, dtype=jnp.int32)
-    low, high, both = tbit ^ 1, tbit ^ 2, tbit ^ 3
-    group = tbit // 2
-
-    def wide(values):
-        return jnp.broadcast_to(values, (A0, 2, 2, R)).reshape(A0, 256)
-
-    def both_sources(values, axis, first, second):
-        return jnp.stack(
-            [by_parent(values, axis, *first), by_parent(values, axis, *second)], axis=2
-        )
-
-    own, other = (tbit, tbit), (both, low)
-    first_slots = ((tbit, tbit), (low, low))
-    other_slots = ((high, tbit), (both, low))
-    row0 = both_sources(points_first, 2, (tbit, tbit), (low, both)).reshape(A0, 256)
-    row1 = both_sources(points_second, 2, *first_slots).reshape(A0, 256)
-    row2 = both_sources(points_second, 2, *other_slots).reshape(A0, 256)
-    row3 = jnp.concatenate(
-        [by_parent(points_third, 2, *side).reshape(A0, 128) for side in (own, other)], axis=1
-    )
-    mine, by_low, by_high, by_both = ranks
-
-    def halves(even, odd):
-        return jnp.concatenate([even[:HALF_A], odd[HALF_A:]], axis=0)
-
-    row4 = wide(jnp.stack([mine[0], by_low[0]], axis=2)[..., None])
-    row5 = wide(
-        jnp.stack([halves(by_high[0], mine[0]), halves(by_both[0], by_low[0])], axis=2)[..., None]
-    )
-    row6 = wide(mine[1][:, :, None, None])
-    row7 = wide(halves(by_both[1], by_low[1])[:, :, None, None])
-    columns = jnp.stack([row0, row1, row2, row3, row4, row5, row6, row7], axis=1)
-
-    targets_first = (
-        jnp.arange(2 * A0, dtype=jnp.int32)[:, None] * (NPTS // (2 * A0)) + checks_first
-    ).reshape(A0, 2, R)
-    targets_second = (
-        jnp.arange(4 * A0, dtype=jnp.int32)[:, None] * (NPTS // (4 * A0)) + checks_second
-    ).reshape(A0, 4, R)
-    targets_third = (
-        jnp.arange(8 * A0, dtype=jnp.int32)[:, None] * (NPTS // (8 * A0)) + checks_third
-    ).reshape(A0, 4, 2 * R)
-    ranks_mine = lax.dynamic_index_in_dim(ranks_third, box, 3, keepdims=False)
-    rows, limits = [], []
-    for side, groups in ((own, (group, group)), (other, (1 - group, group))):
-        rows.append(
-            jnp.concatenate(
-                [by_parent(targets_first, 1, *groups), by_parent(targets_second, 1, *side)],
-                axis=1,
-            )
-            * 4096
-        )
-        rows.append(by_parent(targets_third, 1, *side) * 4096)
-        limit = by_parent(ranks_mine, 1, *side)
-        limits += [jnp.broadcast_to(limit[:, t : t + 1], (A0, LANES)) for t in range(2)]
-    return columns, jnp.stack(rows + limits, axis=1)
-
-
 def per_device(
     coeffs,
     skeleton_first,
@@ -525,11 +526,12 @@
     even, odd, ranks = lax.optimization_barrier((even, odd, ranks))
     near_even = crossed(even, 1)
     near_odd = crossed(odd, 3)
-    columns, rows = tables(
-        tbit, box, skeleton_first, skeleton_second, skeleton_third,
-        checks_first, checks_second, checks_third, ranks, ranks_third,
-    )
-    high, low = build_operators(columns, rows, interpolants)
+    limits = lax.dynamic_index_in_dim(ranks_third, box, 3, keepdims=False)
+    high, low = build_operators(
+        jnp.stack(ranks).reshape(-1), limits.reshape(-1),
+        skeleton_first, skeleton_second, skeleton_third,
+        checks_first, checks_second, checks_third, interpolants,
+    )
     slot_parent, slot_used = slot_table(
         lax.dynamic_index_in_dim(owners, tbit, 0, keepdims=False), 32, CAP
     )

time: 306 us -> 293 us (0.958)
  other arithmetic: 6.96 us -> 1.42 us
  local copies, waits for them, and re-layouts: 27.4 us -> 22.2 us
    another operation x19 -> x1, local copies, waits for them, and re-layouts: 4.49 us -> 0.15 us  [per_device(): jnp.stack(ranks).reshape(-1)]
    add x6 -> x0, other arithmetic: 4.28 us -> none  [the longest x1 1.06 us: tables(): points_third = local_boxes * (NPTS // 64) + skeleton_third]
    unnamed x7 -> x14, local copies, waits for them, and re-layouts: 13.6 us -> 14.2 us
  transfers between devices with their start and end apart: 5 -> 5, of which waited for: 2 -> 2; matrix products, arithmetic and copies ran while one was open for 6% -> 4% of each run, Pallas kernels for 12% -> 13%
where the time goes in v3:
time: 293 us; the launch traced here: 291 us
  Pallas kernels  256 us (87%)
  local copies, waits for them, and re-layouts  22.2 us (8%)
  starting transfers between devices  7.19 us (2%)
  waiting for transfers between devices  4.09 us (1%)
    pallas_call x1, Pallas kernels, exchange(): pl.pallas_call(exchange_kernel, out_shape=jax.ShapeDtypeStruct((2, CAP, 3...  219 us
    pallas_call x1, Pallas kernels, build_operators(): pl.pallas_call(operators_kernel, grid=(A0 // GROUP,), out_shape=(shape, s...  37.3 us
    unnamed x14, local copies, waits for them, and re-layouts  14.2 us
    ppermute x5, starting transfers between devices, crossed(): return lax.ppermute(value, 'tbit', [(k, k ^ mask) for k in range(4)])  7.19 us
  transfers between devices with their start and end apart: 5, of which 2 were waited for; matrix products, arithmetic and copies ran while one was open for 4% of the time, Pallas kernels for 13%

profile of v3, /device:TPU:1, one launch (start us, length us, event | category | flops | bytes accessed | tf_op | source)
XLA Modules:
  0.0 291.2 jit_solution(2797310521191846469)
XLA Ops:
  0.0 0.7 pad_add_fusion.1
  0.8 3.3 %collective-permute-start.2 = (s32[2,64,2]{1,2,0:T(2,128)S(1)}, s32[2,64,2]{1,2,0:T(2,128)S(1)}, u32[]{:S(2)}, u32[]{:S(2)}) collective-permute-start(s32[2,64,2]{1,2,0:T(2,128)S(1)} %pad_add_fusion.1), channel_id=1, source_target_pairs={{0,96},{32,64},{64,32},{96,0},{1,97},{33,65},{65,33},{97,1},{2,98}... | collective-permute-start | bytes 3080 | tf_op jit(solution)/shard_map/ppermute | solution.py:521
  4.1 0.5 collective-permute-start.1
  4.6 0.1 collective-permute-start
  4.7 0.7 dynamic-slice_bitcast_fusion
  5.4 0.1 fusion.1
  5.4 0.1 reduce_window_sum.11
  5.5 0.2 select_reduce_fusion
  5.7 4.0 %fusion.2 = (f32[32,2,64,128]{3,2,1,0:T(8,128)S(1)}, f32[32,2,64,128]{3,2,1,0:T(8,128)}) fusion(f32[64,2,64,256]{3,2,1,0:T(8,128)} %bitcast.15), kind=kLoop, calls=%fused_computation.13 | loop fusion | bytes 8388608 | tf_op jit(solution)/shard_map/slice | solution.py:525
  9.7 0.1 fusion
  9.9 0.2 and_reduce_fusion
  10.1 0.1 copy.27
  10.1 0.7 reshape.64.used
  10.8 0.1 copy.26
  10.9 0.6 reshape.63.parents
  11.6 0.7 copy.23.checks1
  12.3 0.0 collective-permute-done.2
  12.3 0.0 collective-permute-done.1
  12.3 1.5 collective-permute-start.3
  13.8 1.8 collective-permute-start.4
  15.6 0.1 copy.22
  15.8 0.7 reshape.62.limits
  16.5 0.8 copy.24.checks2
  17.3 0.9 copy.25.checks3
  18.2 0.2 copy.21
  18.3 0.8 reshape.61.ranks
  19.1 37.3 %shard_map.118 = (bf16[64,2,128,256]{3,2,1,0:T(8,128)(2,1)}, bf16[64,2,128,256]{3,2,1,0:T(8,128)(2,1)}) custom-call(s32[1024]{0:T(1024)} %reshape.61.ranks, s32[512]{0:T(512)} %reshape.62.limits, s32[64,2,4,64]{3,2,1,0:T(4,128)} %first_ref.1, s32[64,2,4,64]{3,2,1,0:T(4,128)} %second_ref.1, s32[64,2,4,64]{3,2,1,0:T(4,128)} %third_ref.1, ...), custom_call_target="tpu_custom_call" | custom-call | flops 20000000000 | bytes 17000000 | tf_op jit(solution)/shard_map/pallas_call | solution.py:234
  56.4 1.8 collective-permute-done.3.near_even
  58.2 2.2 collective-permute-done.4.near_odd
  60.5 218.8 %shard_map.119 = f32[2,4,32,64,256]{4,3,2,1,0:T(8,128)} custom-call(f32[64,2,64,256]{3,2,1,0:T(8,128)} %bitcast.16, f32[32,2,64,128]{3,2,1,0:T(8,128)} %collective-permute-done.3.near_even, f32[32,2,64,128]{3,2,1,0:T(8,128)} %collective-permute-done.4.near_odd, bf16[64,2,128,256]{3,2,1,0:T(8,128)(2,1)} %get-tuple-element.19.high, ...), custom_call_target="tpu_custom_call" | custom-call | tf_op jit(solution)/shard_map/pallas_call | solution.py:462
  279.3 0.0 copy-start.1
  279.3 11.8 %copy.29 = f32[1,1,2,4,32,64,256]{6,5,4,3,2,1,0:T(8,128)} copy(f32[1,1,2,4,32,64,256]{6,5,4,3,2,1,0:T(8,128)} %bitcast.14) | data formatting | bytes 33554432
  (15 shorter events, 0.1 us)
Async XLA Ops:
  0.0 15.6 %copy-start = (s32[64,4,2,32]{0,3,2,1:T(8,128)S(1)}, s32[64,4,2,32]{0,3,2,1:T(8,128)}, u32[]{:S(2)}) copy-start(s32[64,4,2,32]{0,3,2,1:T(8,128)} %param.21) | copy-start | bytes 196612
  0.0 11.6 %copy-start.4 = (s32[128,64]{0,1:T(8,128)S(1)}, s32[128,64]{0,1:T(8,128)}, u32[]{:S(2)}) copy-start(s32[128,64]{0,1:T(8,128)} %param.16) | copy-start | bytes 98308
  0.0 16.5 %copy-start.3 = (s32[256,64]{0,1:T(8,128)S(1)}, s32[256,64]{0,1:T(8,128)}, u32[]{:S(2)}) copy-start(s32[256,64]{0,1:T(8,128)} %param.17) | copy-start | bytes 196612
  0.0 17.3 %copy-start.2 = (s32[512,64]{0,1:T(8,128)S(1)}, s32[512,64]{0,1:T(8,128)}, u32[]{:S(2)}) copy-start(s32[512,64]{0,1:T(8,128)} %param.18) | copy-start | bytes 393220
  0.8 11.6 %collective-permute-start.2 = (s32[2,64,2]{1,2,0:T(2,128)S(1)}, s32[2,64,2]{1,2,0:T(2,128)S(1)}, u32[]{:S(2)}, u32[]{:S(2)}) collective-permute-start(s32[2,64,2]{1,2,0:T(2,128)S(1)} %pad_add_fusion.1), channel_id=1, source_target_pairs={{0,96},{32,64},{64,32},{96,0},{1,97},{33,65},{65,33},{97,1},{2,98}... | collective-permute-start | bytes 3080 | tf_op jit(solution)/shard_map/ppermute | solution.py:521
  4.1 8.2 %collective-permute-start.1 = (s32[2,64,2]{1,2,0:T(2,128)S(1)}, s32[2,64,2]{1,2,0:T(2,128)S(1)}, u32[]{:S(2)}, u32[]{:S(2)}) collective-permute-start(s32[2,64,2]{1,2,0:T(2,128)S(1)} %pad_add_fusion.1), channel_id=1, source_target_pairs={{0,64},{32,96},{64,0},{96,32},{1,65},{33,97},{65,1},{97,33},{2,66}... | collective-permute-start | bytes 3080 | tf_op jit(solution)/shard_map/ppermute | solution.py:521
  4.6 7.7 %collective-permute-start = (s32[2,64,2]{1,2,0:T(2,128)S(1)}, s32[2,64,2]{1,2,0:T(2,128)S(1)}, u32[]{:S(2)}, u32[]{:S(2)}) collective-permute-start(s32[2,64,2]{1,2,0:T(2,128)S(1)} %pad_add_fusion.1), channel_id=1, source_target_pairs={{0,32},{32,0},{64,96},{96,64},{1,33},{33,1},{65,97},{97,65},{2,34}... | collective-permute-start | bytes 3080 | tf_op jit(solution)/shard_map/ppermute | solution.py:521
  12.3 45.9 %collective-permute-start.3 = (f32[32,2,64,128]{3,2,1,0:T(8,128)}, f32[32,2,64,128]{3,2,1,0:T(8,128)}, u32[]{:S(2)}, u32[]{:S(2)}) collective-permute-start(f32[32,2,64,128]{3,2,1,0:T(8,128)} %get-tuple-element.13), channel_id=1, source_target_pairs={{0,32},{32,0},{64,96},{96,64},{1,33},{33,1},{65,97},{97,65},{2,34}... | collective-permute-start | bytes 6291464 | tf_op jit(solution)/shard_map/ppermute | solution.py:521
  13.8 46.6 %collective-permute-start.4 = (f32[32,2,64,128]{3,2,1,0:T(8,128)S(1)}, f32[32,2,64,128]{3,2,1,0:T(8,128)}, u32[]{:S(2)}, u32[]{:S(2)}) collective-permute-start(f32[32,2,64,128]{3,2,1,0:T(8,128)S(1)} %get-tuple-element.14), channel_id=1, source_target_pairs={{0,96},{32,64},{64,32},{96,0},{1,97},{33,65},{65,33},{97,1},{2,98}... | collective-permute-start | bytes 6291464 | tf_op jit(solution)/shard_map/ppermute | solution.py:521
  279.3 11.9 %copy-start.1 = (s32[64,4,2,32]{0,3,2,1:T(8,128)S(1)}, s32[64,4,2,32]{0,3,2,1:T(8,128)}, u32[]{:S(2)}) copy-start(s32[64,4,2,32]{0,3,2,1:T(8,128)} %param.21) | copy-start | bytes 196612
